TPU v7x, 256 devices: a whole 4x4x8 slice. The times are simulated.
256 devices in a mesh: seq: 16 (over z, core), head: 16 (over y, x).
Axes of the slice: x: 4, y: 4, z: 8, core: 2. Of those that a mesh axis runs over, the one named last changes fastest.
Arguments:
- queries: bfloat16 [49152, 32, 128], P('seq', 'head'), may hold values from -6 to 6
- keys: bfloat16 [49152, 32, 128], P('seq', 'head'), may hold values from -6 to 6
- values: bfloat16 [49152, 32, 128], P('seq', 'head'), may hold values from -60 to 60
- cotangent: bfloat16 [49152, 32, 128], P('seq', 'head'), may hold values from -6 to 6
- doc_lengths: int32 [6], replicated, may hold values from 1 to 36864, 49152 in all
Outputs:
- output: bfloat16 [49152, 32, 128], P('seq', 'head')
- grad_queries: bfloat16 [49152, 32, 128], P('seq', 'head')
- grad_keys: bfloat16 [49152, 32, 128], P('seq', 'head')
- grad_values: bfloat16 [49152, 32, 128], P('seq', 'head')
All inputs are finite; a program needn't handle non-finite values.
Results may differ from a plain program's by a relative error of at most 0.0058.
Values sent between devices are 32-bit elements; how exact they have to be, the bound alone decides.
A program may use at most 128 MiB of HBM per device.

v0:
```python
import jax
import jax.numpy as jnp
from jax import lax
from jax.sharding import PartitionSpec as P

GROUP = 256


EPSILON = 1e-06


def carried_in(value, axis, join, neutral, backward):
    count, mine = (lax.axis_size(axis), lax.axis_index(axis))
    pieces = jax.tree.map(lambda part: lax.all_gather(part, axis), value)
    if backward:
        pieces = jax.tree.map(lambda part: part[::-1], pieces)
        mine = count - 1 - mine
    total = jax.tree.map(
        lambda part, zero: jnp.full_like(part, 0) + jnp.asarray(zero, part.dtype), value, neutral
    )

    def turn(position, total):
        longer = join(total, jax.tree.map(lambda part: part[position], pieces))
        return jax.tree.map(lambda new, old: jnp.where(position < mine, new, old), longer, total)

    return lax.fori_loop(0, count - 1, turn, total)


def segment_of(places, doc_ends):
    return jnp.sum((doc_ends[None, :] <= places[:, None]).astype(jnp.int32), axis=1)


def chain_join(earlier, later):
    return (later[0] + (1.0 - later[1][0]) * earlier[0], jnp.maximum(earlier[1], later[1]))


def group_prefix(running, inputs):
    added, keeping = inputs
    return (jnp.where(keeping, running, 0.0) + added, running)


def per_device(queries, keys, values, cotangent, doc_lengths):
    tokens_here, heads_here, head_width = queries.shape
    n_groups = tokens_here // GROUP
    device_index = lax.axis_index("seq")
    width_all = float(heads_here * lax.axis_size("head") * head_width)
    doc_ends = jnp.cumsum(doc_lengths)
    anchor = device_index * tokens_here
    positions = anchor + jnp.arange(tokens_here, dtype=jnp.int32)
    segment = segment_of(positions, doc_ends).reshape(n_groups, GROUP)
    group_first = anchor + jnp.arange(n_groups, dtype=jnp.int32) * GROUP
    before_group = segment_of(group_first - 1, doc_ends)
    after_group = segment_of(group_first + GROUP, doc_ends)
    edges = segment_of(jnp.stack([anchor - 1, anchor + tokens_here]), doc_ends)
    before_shard = edges[0]
    after_shard = edges[1]

    def blocks(array):
        return array.reshape(n_groups, GROUP, heads_here, head_width)

    query_blocks = blocks(queries)
    key_blocks = blocks(keys)
    value_blocks = blocks(values)
    grad_blocks = blocks(cotangent)
    causal = jnp.arange(GROUP)[:, None] >= jnp.arange(GROUP)[None, :]
    within = causal[None] & (segment[:, :, None] == segment[:, None, :])
    scores = jnp.einsum(
        "nthd,nshd->nhts", query_blocks, key_blocks, preferred_element_type=jnp.float32
    )
    probs = jnp.where(within[:, None], scores, 0.0).astype(jnp.bfloat16)
    mixed = jnp.einsum("nhts,nshd->nthd", probs, value_blocks, preferred_element_type=jnp.float32)
    tail = (segment == segment[:, -1:]).astype(jnp.bfloat16)[:, :, None, None]
    group_sums = jnp.einsum(
        "nthi,nthj->nhij", key_blocks * tail, value_blocks, preferred_element_type=jnp.float32
    )
    keep_forward = segment[:, -1] == before_group
    zero_state = jnp.zeros((heads_here, head_width, head_width), jnp.float32)
    zero_flag = jnp.zeros((1,), jnp.float32)
    shard_state, local_states = lax.scan(group_prefix, zero_state, (group_sums, keep_forward))
    flag_forward = (segment[-1, -1] != before_shard).astype(jnp.float32).reshape(1)
    remote_state, _ = carried_in(
        (shard_state, flag_forward), "seq", chain_join, (zero_state, zero_flag), False
    )
    local_bf = local_states.astype(jnp.bfloat16)
    remote_bf = remote_state.astype(jnp.bfloat16)
    gate_local = (segment == before_group[:, None]).astype(jnp.float32)[:, :, None, None]
    gate_remote = (segment == before_shard).astype(jnp.float32)[:, :, None, None]
    mixed = mixed + gate_local * jnp.einsum(
        "nthi,nhij->nthj", query_blocks, local_bf, preferred_element_type=jnp.float32
    )
    mixed = mixed + gate_remote * jnp.einsum(
        "nthi,hij->nthj", query_blocks, remote_bf, preferred_element_type=jnp.float32
    )
    squares = jnp.sum(mixed * mixed, axis=(2, 3))
    grad_in = grad_blocks.astype(jnp.float32)
    total_squares = lax.psum(squares, "head")
    root = jnp.sqrt(total_squares / width_all + EPSILON)
    normed = mixed / root[:, :, None, None]
    centre = lax.psum(jnp.sum(grad_in * normed, axis=(2, 3)), "head") / width_all
    output = normed.astype(jnp.bfloat16).reshape(tokens_here, heads_here, head_width)
    grad_mixed = ((grad_in - normed * centre[:, :, None, None]) / root[:, :, None, None]).astype(
        jnp.bfloat16
    )
    grad_probs = jnp.where(
        within[:, None],
        jnp.einsum("nthd,nshd->nhts", grad_mixed, value_blocks, preferred_element_type=jnp.float32),
        0.0,
    ).astype(jnp.bfloat16)
    grad_query = jnp.einsum(
        "nhts,nshd->nthd", grad_probs, key_blocks, preferred_element_type=jnp.float32
    )
    grad_query = grad_query + gate_local * jnp.einsum(
        "nthj,nhij->nthi", grad_mixed, local_bf, preferred_element_type=jnp.float32
    )
    grad_query = grad_query + gate_remote * jnp.einsum(
        "nthj,hij->nthi", grad_mixed, remote_bf, preferred_element_type=jnp.float32
    )
    head_part = (segment == segment[:, :1]).astype(jnp.bfloat16)[:, :, None, None]
    group_back = jnp.einsum(
        "nthi,nthj->nhij", query_blocks * head_part, grad_mixed, preferred_element_type=jnp.float32
    )
    keep_backward = segment[:, 0] == after_group
    shard_back, local_back = lax.scan(
        group_prefix, zero_state, (group_back, keep_backward), reverse=True
    )
    flag_backward = (segment[0, 0] != after_shard).astype(jnp.float32).reshape(1)
    remote_back, _ = carried_in(
        (shard_back, flag_backward), "seq", chain_join, (zero_state, zero_flag), True
    )
    back_local_bf = local_back.astype(jnp.bfloat16)
    back_remote_bf = remote_back.astype(jnp.bfloat16)
    later_local = (segment == after_group[:, None]).astype(jnp.float32)[:, :, None, None]
    later_remote = (segment == after_shard).astype(jnp.float32)[:, :, None, None]
    grad_key = jnp.einsum(
        "nhts,nthd->nshd", grad_probs, query_blocks, preferred_element_type=jnp.float32
    )
    grad_key = grad_key + later_local * jnp.einsum(
        "nshj,nhij->nshi", value_blocks, back_local_bf, preferred_element_type=jnp.float32
    )
    grad_key = grad_key + later_remote * jnp.einsum(
        "nshj,hij->nshi", value_blocks, back_remote_bf, preferred_element_type=jnp.float32
    )
    grad_value = jnp.einsum(
        "nhts,nthd->nshd", probs, grad_mixed, preferred_element_type=jnp.float32
    )
    grad_value = grad_value + later_local * jnp.einsum(
        "nshi,nhij->nshj", key_blocks, back_local_bf, preferred_element_type=jnp.float32
    )
    grad_value = grad_value + later_remote * jnp.einsum(
        "nshi,hij->nshj", key_blocks, back_remote_bf, preferred_element_type=jnp.float32
    )
    shape = (tokens_here, heads_here, head_width)
    return (
        output,
        grad_query.astype(jnp.bfloat16).reshape(shape),
        grad_key.astype(jnp.bfloat16).reshape(shape),
        grad_value.astype(jnp.bfloat16).reshape(shape),
    )


def solution(mesh):
    return jax.shard_map(
        per_device,
        mesh=mesh,
        in_specs=(
            P("seq", "head", None),
            P("seq", "head", None),
            P("seq", "head", None),
            P("seq", "head", None),
            P(),
        ),
        out_specs=(
            P("seq", "head", None),
            P("seq", "head", None),
            P("seq", "head", None),
            P("seq", "head", None),
        ),
        check_vma=False,
    )
```

profile of v0, /device:TPU:0, one launch (start us, length us, event | category | flops | bytes accessed | tf_op | source)
XLA Modules:
  0.0 447.0 jit_solution(13010664251563650226)
XLA Ops:
  9.3 3.5 copy.177
  14.2 1.7 fusion.7
  17.0 34.0 %while.58 = (s32[]{:T(128)}, f32[2,128,128]{2,1,0:T(8,128)S(1)}, bf16[12,2,128,128]{3,2,1,0:T(8,128)(2,1)}, pred[12]{0:T(512)(128)(4,1)S(1)}, f32[12,2,128,128]{3,2,1,0:T(8,128)}, /*index=5*/s32[]{:T(128)}, s32[]{:T(128)}) while((s32[]{:T(128)}, f32[2,128,128]{2,1,0:T(8,128)S(1)}, bf16[12,2,128,128]{3,2,1,0:T(8,128)(2,1)}, ...), condition=%wide.region_4.5_spmd.clone, body=%wide.region_3.4_spmd.clone.sunk | while | flops 131075 | bytes 590435 | solution.py:79
  18.2 1.6 bitcast_add_fusion.13
  21.0 1.6 bitcast_add_fusion.13
  23.8 1.6 bitcast_add_fusion.13
  26.7 1.6 bitcast_add_fusion.13
  32.3 1.6 bitcast_add_fusion.13
  35.2 1.6 bitcast_add_fusion.13
  54.8 4.8 %copy.197 = bf16[12,256,2,128]{1,3,2,0:T(8,128)(2,1)} copy(bf16[12,256,2,128]{3,2,1,0:T(2,128)(2,1)} %bitcast.144) | data formatting | bytes 3145728 | tf_op jit(solution)/shard_map/reshape | solution.py:59
  59.6 2.8 copy.186
  64.3 27.9 %all-reduce.2 = (f32[16]{0:T(128)S(1)}, f32[16]{0:T(128)S(1)}) all-reduce(f32[16]{0:T(128)S(1)} %dynamic-update-slice, f32[16]{0:T(128)S(1)} %dynamic-update-slice.1), channel_id=1, replica_groups=mesh['seq'=16,'head'=16] {'seq'}, use_global_device_ids=true, to_apply=%add | all-reduce | flops 32 | bytes 256
  93.0 2.7 select_convert_fusion.1
  95.7 1.6 copy-done.8
  97.4 2.6 fusion.14
  100.0 33.4 %while.59 = (s32[]{:T(128)}, f32[2,128,128]{2,1,0:T(8,128)S(1)}, s32[]{:T(128)}, f32[16,2,128,128]{3,2,1,0:T(8,128)}, f32[16,1]{0,1:T(1,128)S(1)}, /*index=5*/s32[]{:T(128)}, s32[]{:T(128)}) while((s32[]{:T(128)}, f32[2,128,128]{2,1,0:T(8,128)S(1)}, s32[]{:T(128)}, f32[16,2,128,128]{3,2,1,0:T(8,128)}, f32[16,1]{0,1:T(1,128)S(1)}, ...), condition=%wide.region_7.8_spmd.clone, body=%wide.region_6.7_spmd.clone.sunk | while | flops 131077 | bytes 393333 | solution.py:26
  100.6 1.6 fusion.73
  102.8 1.6 fusion.73
  105.0 1.6 fusion.73
  107.3 1.6 fusion.73
  109.5 1.6 fusion.73
  111.7 1.6 fusion.73
  114.0 1.6 fusion.73
  116.2 1.6 fusion.73
  118.4 1.6 fusion.73
  120.6 1.6 fusion.73
  122.9 1.6 fusion.73
  125.1 1.6 fusion.73
  127.3 1.6 fusion.73
  129.5 1.6 fusion.73
  131.8 1.6 fusion.73
  133.4 2.3 fusion.27
  136.3 4.7 %multiply_reduce_fusion.1 = (f32[12,256]{1,0:T(8,128)S(1)}, f32[12,256,2,128]{3,1,2,0:T(8,128)}) fusion(f32[2,128,12,256]{1,3,0,2:T(8,128)S(1)} %fusion.27, f32[12,256]{1,0:T(8,128)S(1)} %get-tuple-element.468, bf16[12,256,2,128]{1,3,2,0:T(8,128)(2,1)S(1)} %copy-done.1, bf16[12,2,128,128]{3,2,1,0:T(8,128)(2,1)} %get-tuple-element.324, ...), kind=kOutput, calls=%fused_computation.24 | convolution fusion | flops 206042112 | bytes 11833344 | tf_op jit(solution)/shard_map/nthi,nhij->nthj/dot_general | solution.py:88
  140.9 75.0 %psum.14 = f32[12,256]{1,0:T(8,128)S(1)} all-reduce(f32[12,256]{1,0:T(8,128)S(1)} %get-tuple-element.476), channel_id=1, replica_groups=mesh['seq'=16,'head'=16] {'head'}, use_global_device_ids=true, to_apply=%region_9.10 | all-reduce | flops 3072 | bytes 24576 | tf_op jit(solution)/shard_map/psum | solution.py:96
  216.0 2.9 multiply_reduce_fusion
  218.8 69.7 %psum.15 = f32[12,256]{1,0:T(8,128)S(1)} all-reduce(f32[12,256]{1,0:T(8,128)S(1)} %multiply_reduce_fusion), channel_id=1, replica_groups=mesh['seq'=16,'head'=16] {'head'}, use_global_device_ids=true, to_apply=%region_11.12 | all-reduce | flops 3072 | bytes 24576 | tf_op jit(solution)/shard_map/psum | solution.py:99
  288.6 3.8 divide_convert_fusion
  292.4 1.7 fusion.5
  295.2 32.7 %while.60 = (s32[]{:T(128)}, f32[2,128,128]{2,1,0:T(8,128)S(1)}, bf16[12,2,128,128]{3,2,1,0:T(8,128)(2,1)}, pred[12]{0:T(512)(128)(4,1)S(1)}, f32[12,2,128,128]{...) while((s32[]{:T(128)}, f32[2,128,128]{2,1,0:T(8,128)S(1)}, ...), condition=%wide.region_14.15_spmd.clone, body=%wide.region_13.14_spmd.clone.sunk | while | flops 131076 | bytes 589947 | solution.py:123
  328.7 2.4 fusion.44
  334.4 13.8 %copy.213 = bf16[3072,2,128]{2,1,0:T(2,128)(2,1)} copy(bf16[3072,2,128]{2,0,1:T(8,128)(2,1)S(1)} %bitcast.138) | data formatting | bytes 3145728
  348.3 14.0 %copy.212 = bf16[3072,2,128]{2,1,0:T(2,128)(2,1)} copy(bf16[3072,2,128]{2,0,1:T(8,128)(2,1)S(1)} %bitcast.139) | data formatting | bytes 3145728
  362.4 2.2 fusion.10
  365.1 2.7 fusion.43
  367.8 2.7 fusion.42
  370.5 3.2 rev.6
  373.8 33.4 %while.61 = (s32[]{:T(128)}, f32[2,128,128]{2,1,0:T(8,128)S(1)}, s32[]{:T(128)}, f32[16,2,128,128]{3,2,1,0:T(8,128)}, f32[16,1]{0,1:T(1,128)S(1)}, /*index=5*/s32[]{:T(128)}, s32[]{:T(128)}) while((s32[]{:T(128)}, f32[2,128,128]{2,1,0:T(8,128)S(1)}, s32[]{:T(128)}, f32[16,2,128,128]{3,2,1,0:T(8,128)}, f32[16,1]{0,1:T(1,128)S(1)}, ...), condition=%wide.region_16.17_spmd.clone, body=%wide.region_15.16_spmd.clone.sunk | while | flops 131077 | bytes 393333 | solution.py:26
  374.3 1.6 fusion.75
  376.6 1.6 fusion.75
  378.8 1.6 fusion.75
  381.0 1.6 fusion.75
  383.3 1.6 fusion.75
  385.5 1.6 fusion.75
  387.7 1.6 fusion.75
  389.9 1.6 fusion.75
  392.2 1.6 fusion.75
  394.4 1.6 fusion.75
  396.6 1.6 fusion.75
  398.9 1.6 fusion.75
  401.1 1.6 fusion.75
  403.3 1.6 fusion.75
  405.5 1.6 fusion.75
  411.0 14.0 %copy.215 = bf16[3072,2,128]{2,1,0:T(2,128)(2,1)} copy(bf16[3072,2,128]{2,0,1:T(8,128)(2,1)S(1)} %bitcast.140) | data formatting | bytes 3145728
  426.4 13.8 %copy.214 = bf16[3072,2,128]{2,1,0:T(2,128)(2,1)} copy(bf16[3072,2,128]{2,0,1:T(8,128)(2,1)S(1)} %bitcast.141) | data formatting | bytes 3145728
  (181 shorter events, 94.1 us)
Async XLA Ops:
  7.2 7.0 %copy-start = (bf16[3072,2,128]{2,1,0:T(2,128)(2,1)S(1)}, bf16[3072,2,128]{2,1,0:T(2,128)(2,1)}, u32[]{:S(2)}) copy-start(bf16[3072,2,128]{2,1,0:T(2,128)(2,1)} %param.15) | copy-start | bytes 4718596
  7.2 92.8 %all-gather.5.cloned.1.call-start = ((), (), s32[]{:S(2)}) async-start(), calls=%async_computation | async-start | bytes 2228224 | tf_op jit(solution)/shard_map/all_gather | solution.py:14
  50.9 0.7 copy-start.7
  51.6 318.9 %all-gather.7.cloned.1.call-start = ((), (), s32[]{:S(2)}) async-start(), calls=%async_computation.1 | async-start | bytes 2228224 | tf_op jit(solution)/shard_map/all_gather | solution.py:14
  59.6 2.8 copy-start.19
  93.0 2.7 copy-start.17
  95.7 1.6 copy-start.8
  133.4 2.3 copy-start.1
  133.4 2.8 copy-start.13
  288.6 3.8 copy-start.2
  292.4 1.7 copy-start.4
  327.9 0.7 copy-start.6
  328.7 2.4 copy-start.5
  328.7 2.4 copy-start.18
  334.4 13.8 %copy-start.16 = (bf16[12,256,2,128]{3,1,2,0:T(8,128)(2,1)S(1)}, bf16[12,256,2,128]{3,1,2,0:T(8,128)(2,1)}, u32[]{:S(2)}) copy-start(bf16[12,256,2,128]{3,1,2,0:T(8,128)(2,1)} %get-tuple-element.465) | copy-start | bytes 4718596
  348.3 14.0 %copy-start.14 = (bf16[12,2,128,128]{3,2,1,0:T(8,128)(2,1)S(1)}, bf16[12,2,128,128]{3,2,1,0:T(8,128)(2,1)}, u32[]{:S(2)}) copy-start(bf16[12,2,128,128]{3,2,1,0:T(8,128)(2,1)} %get-tuple-element.327) | copy-start | bytes 2359300
  362.4 2.7 copy-start.9
  365.1 2.7 copy-start.3
  407.2 1.9 copy-start.12
  407.2 2.1 copy-start.15
  410.8 14.2 %copy-start.11 = (f32[12,2,256,128]{3,2,1,0:T(8,128)S(1)}, f32[12,2,256,128]{3,2,1,0:T(8,128)}, u32[]{:S(2)}) copy-start(f32[12,2,256,128]{3,2,1,0:T(8,128)} %fusion.42) | copy-start | bytes 9437188
  411.0 14.1 %copy-start.10 = (f32[12,2,128,256]{2,3,1,0:T(8,128)S(1)}, f32[12,2,128,256]{2,3,1,0:T(8,128)}, u32[]{:S(2)}) copy-start(f32[12,2,128,256]{2,3,1,0:T(8,128)} %fusion.10) | copy-start | bytes 9437188
Sparse Core Ops, SparseCore 0:
  51.7 40.5 all-gather.4
  328.7 31.5 all-gather.6
where the time goes:
time: 449 us; the launch traced here: 447 us
  blocking collectives  173 us (39%)
  other arithmetic  129 us (29%)
  local copies, waits for them, and re-layouts  94.9 us (21%)
  matrix products  32.5 us (7%)
  between operations  16.9 us (4%)
    psum x1, blocking collectives, per_device(): total_squares = lax.psum(squares, 'head')  75 us
    psum x1, blocking collectives, per_device(): lax.psum(jnp.sum(grad_in * normed, axis=(2, 3)), 'head') / width_all  69.7 us
    unnamed x51, local copies, waits for them, and re-layouts  65.7 us
    select_n x30, other arithmetic, turn(): jnp.where(position < mine, new, old)  48.8 us
    add x24, other arithmetic, group_prefix(): return (jnp.where(keeping, running, 0.0) + added, running)  37.3 us
    unnamed x1, blocking collectives  27.9 us
    sub x30, other arithmetic, chain_join(): 1.0 - later[1][0]  17.6 us
    dynamic_update_slice x24, other arithmetic, per_device(): lax.scan(group_prefix, zero_state, (group_sums, keep_forward))  15.2 us
  transfers between devices with their start and end apart: 2, of which 0 were waited for; matrix products, arithmetic and copies ran while one was open for 13% of the time, Pallas kernels for 0%

commit v1 on v0

v1 whole, which is shorter than its diff:
```python
import functools

import jax
import jax.numpy as jnp
from jax import lax
from jax.experimental import pallas as pl
from jax.experimental.pallas import tpu as pltpu
from jax.sharding import PartitionSpec as P

GROUP = 256
EPSILON = 1e-06
MESH = pl.DeviceIdType.MESH
F32 = jnp.float32
BF16 = jnp.bfloat16


def dot(a, b, ca=1, cb=0):
    return lax.dot_general(a, b, (((ca,), (cb,)), ((), ())), preferred_element_type=F32)


def kernel(
    sizes,
    doc_ref,
    q_hbm,
    k_hbm,
    v_hbm,
    g_hbm,
    out_hbm,
    dq_hbm,
    dk_hbm,
    dv_hbm,
    raw,
    tmp,
    heads,
    mask_ref,
    gates,
    p_ref,
    o_ref,
    dob_ref,
    dkl_ref,
    dvl_ref,
    stage_f,
    stage_b,
    s_loc,
    s_bf,
    r_loc,
    s_run,
    s_got,
    s_pre,
    s_in,
    r_run,
    r_got,
    r_pre,
    r_in,
    part,
    x_got,
    x_sum,
    y_got,
    tot,
    in_sem,
    out_sem,
    s_send,
    s_recv,
    t_send,
    t_recv,
    r_send,
    r_recv,
    u_send,
    u_recv,
    x_send,
    x_recv,
    y_send,
    y_recv,
):
    n_seq, n_x, n_y, n_groups, n_heads = sizes
    tokens = n_groups * GROUP
    rows2 = GROUP * n_heads
    width_all = float(n_x * n_y * n_heads * 128)
    me = lax.axis_index("seq")
    head = lax.axis_index("head")
    mx = lax.rem(head, n_x)
    my = head // n_x
    slab = n_heads * 128 // n_seq

    def head_of(x, y):
        return y * n_x + x

    barrier = pltpu.get_barrier_semaphore()
    for d in range(1, n_seq):
        pl.semaphore_signal(barrier, inc=1, device_id={"seq": lax.rem(me + d, n_seq)}, device_id_type=MESH)
    for d in range(1, n_x):
        pl.semaphore_signal(
            barrier, inc=1, device_id={"head": head_of(lax.rem(mx + d, n_x), my)}, device_id_type=MESH
        )
    for d in range(1, n_y):
        pl.semaphore_signal(
            barrier, inc=1, device_id={"head": head_of(mx, lax.rem(my + d, n_y))}, device_id_type=MESH
        )

    sources = (k_hbm, v_hbm, q_hbm, g_hbm)
    KK, VV, QQ, GG = range(4)

    def load(a, g):
        return pltpu.make_async_copy(sources[a].at[g], raw.at[a, g], in_sem.at[a, g])

    @pl.loop(0, n_groups)
    def _(g):
        load(KK, g).start()
        load(VV, g).start()

    @pl.loop(0, n_groups)
    def _(g):
        load(QQ, g).start()
        load(GG, g).start()

    ends = []
    total = 0
    for j in range(doc_ref.shape[0]):
        total = total + doc_ref[j]
        ends.append(total)

    def seg_of(p):
        s = (ends[0] <= p).astype(jnp.int32)
        for e in ends[1:]:
            s = s + (e <= p).astype(jnp.int32)
        return s

    def flag(cond):
        return jnp.where(cond, 1.0, 0.0).astype(F32)

    shard_first = me * tokens
    bs = seg_of(shard_first - 1)
    after_s = seg_of(shard_first + tokens)

    def edges(g):
        first = shard_first + g * GROUP
        return seg_of(first - 1), seg_of(first), seg_of(first + GROUP - 1), seg_of(first + GROUP)

    GB, GT, GH, GA = range(4)

    @pl.loop(0, n_groups)
    def _(g):
        first = shard_first + g * GROUP
        bc, c0, c1, ac = edges(g)
        row = lax.broadcasted_iota(jnp.int32, (GROUP, 128), 0)
        seg_r = seg_of(row + first)
        col = lax.broadcasted_iota(jnp.int32, (8, GROUP), 1)
        seg_c = seg_of(col + first)[0:1]
        for half in range(2):
            lane = lax.broadcasted_iota(jnp.int32, (GROUP, 128), 1) + half * 128
            same = seg_r == jnp.broadcast_to(seg_c[:, half * 128 : half * 128 + 128], (GROUP, 128))
            mask_ref[g, :, half * 128 : half * 128 + 128] = jnp.where(
                jnp.logical_and(same, row >= lane), 1.0, 0.0
            ).astype(F32)
        for i, ref_seg in ((GB, bc), (GT, c1), (GH, c0), (GA, ac)):
            gates[i, g] = jnp.where(seg_r == ref_seg, 1.0, 0.0).astype(BF16)

    def split(a, g):
        tmp[a] = raw[a, g].astype(F32)
        for h in range(n_heads):
            heads[a, h, g] = tmp[a, pl.ds(h, GROUP, stride=n_heads), :].astype(BF16)

    s_run[...] = jnp.zeros_like(s_run)

    @pl.loop(0, n_groups)
    def _(g):
        bc, c0, c1, ac = edges(g)
        load(KK, g).wait()
        load(VV, g).wait()
        split(KK, g)
        split(VV, g)
        keep = flag(c1 == bc)
        for h in range(n_heads):
            added = dot(heads[KK, h, g] * gates[GT, g], heads[VV, h, g], 0, 0)
            old = s_run[h]
            s_loc[h, g] = old
            s_run[h] = keep * old + added

    pl.semaphore_wait(barrier, n_seq - 1 + n_x - 1 + n_y - 1)

    def hand(src, dst, send, recv, d):
        peer = lax.rem(me + d, n_seq)
        return pltpu.make_async_remote_copy(
            src_ref=src(peer),
            dst_ref=dst,
            send_sem=send.at[d],
            recv_sem=recv.at[me],
            device_id={"seq": peer},
            device_id_type=MESH,
        )

    def arrived(dst, send, recv, d):
        peer = lax.rem(me + d, n_seq)
        return pltpu.make_async_remote_copy(
            src_ref=dst(peer),
            dst_ref=dst(peer),
            send_sem=send.at[d],
            recv_sem=recv.at[peer],
            device_id={"seq": peer},
            device_id_type=MESH,
        )

    def rows(ref, i):
        return ref.at[pl.ds(pl.multiple_of(i * slab, slab), slab)]

    def scatter(run2d, got, send, recv):
        for d in range(1, n_seq):
            hand(lambda p: rows(run2d, p), got.at[me], send, recv, d).start()

    def scatter_done(run2d, got, send, recv):
        for d in range(1, n_seq):
            hand(lambda p: rows(run2d, p), got.at[me], send, recv, d).wait_send()
            arrived(lambda p: got.at[p], send, recv, d).wait_recv()

    def give(pre, into, send, recv):
        for d in range(1, n_seq):
            hand(lambda p: pre.at[p], rows(into, me), send, recv, d).start()

    def give_done(pre, into, send, recv):
        for d in range(1, n_seq):
            hand(lambda p: pre.at[p], rows(into, me), send, recv, d).wait_send()
            arrived(lambda p: rows(into, p), send, recv, d).wait_recv()

    def combine(run2d, got, pre, into, backward):
        got[me] = run2d[pl.ds(pl.multiple_of(me * slab, slab), slab), :]
        carry = jnp.zeros((slab, 128), F32)
        order = range(n_seq - 1, -1, -1) if backward else range(n_seq)
        for i in order:
            pre[i] = carry
            first = i * tokens
            if backward:
                keep = flag(seg_of(first) == seg_of(first + tokens))
            else:
                keep = flag(seg_of(first + tokens - 1) == seg_of(first - 1))
            carry = keep * carry + got[i]
        into[pl.ds(pl.multiple_of(me * slab, slab), slab), :] = pre[me]

    def flat(ref):
        return ref.reshape(n_heads * 128, 128)

    scatter(flat(s_run), s_got, s_send, s_recv)

    def intra(g):
        load(QQ, g).wait()
        split(QQ, g)
        for h in range(n_heads):
            scores = dot(heads[QQ, h, g], heads[KK, h, g], 1, 1)
            probs = (scores * mask_ref[g]).astype(BF16)
            p_ref[h, g] = probs
            o_ref[h, g] = dot(probs, heads[VV, h, g])

    half = n_groups // 2

    @pl.loop(0, half)
    def _(g):
        intra(g)

    scatter_done(flat(s_run), s_got, s_send, s_recv)
    combine(flat(s_run), s_got, s_pre, s_in, False)
    give(s_pre, s_in, t_send, t_recv)

    @pl.loop(half, n_groups)
    def _(g):
        intra(g)

    @pl.loop(0, n_groups)
    def _(g):
        load(GG, g).wait()
        split(GG, g)

    give_done(s_pre, s_in, t_send, t_recv)

    ones = jnp.ones((16, n_heads * 128), BF16)

    @pl.loop(0, n_groups)
    def _(g):
        bc, c0, c1, ac = edges(g)
        w = flag(bc == bs)
        squares, inner = [], []
        for h in range(n_heads):
            state = (s_loc[h, g] + w * s_in[h * 128 : h * 128 + 128, :]).astype(BF16)
            s_bf[h, g] = state
            o = o_ref[h, g] + dot(heads[QQ, h, g] * gates[GB, g], state)
            o_ref[h, g] = o
            squares.append((o * o).astype(BF16))
            inner.append((heads[GG, h, g].astype(F32) * o).astype(BF16))
        part[pl.ds(g, 1), :] = dot(ones, jnp.concatenate(squares, axis=1), 1, 1)[0:1]
        part[pl.ds(n_groups + g, 1), :] = dot(ones, jnp.concatenate(inner, axis=1), 1, 1)[0:1]

    def ring(axis_x, src, got, send, recv, d, wait):
        n, mine = (n_x, mx) if axis_x else (n_y, my)
        other = lax.rem(mine + d, n)
        peer = head_of(other, my) if axis_x else head_of(mx, other)
        slot = other if wait else mine
        return pltpu.make_async_remote_copy(
            src_ref=src,
            dst_ref=got.at[slot],
            send_sem=send.at[d],
            recv_sem=recv.at[slot],
            device_id={"head": peer},
            device_id_type=MESH,
        )

    def reduce_over(axis_x, src, got, send, recv, into):
        n, mine = (n_x, mx) if axis_x else (n_y, my)
        for d in range(1, n):
            ring(axis_x, src, got, send, recv, d, False).start()
        got[mine] = src[...]
        for d in range(1, n):
            ring(axis_x, src, got, send, recv, d, False).wait_send()
            ring(axis_x, src, got, send, recv, d, True).wait_recv()
        value = got[0]
        for i in range(1, n):
            value = value + got[i]
        into[...] = value

    reduce_over(True, part, x_got, x_send, x_recv, x_sum)
    reduce_over(False, x_sum, y_got, y_send, y_recv, tot)

    r_run[...] = jnp.zeros_like(r_run)
    sub = lax.broadcasted_iota(jnp.int32, (16, 256), 0)
    lane = lax.broadcasted_iota(jnp.int32, (16, 256), 1)
    spread = jnp.where(
        jnp.logical_or(
            jnp.logical_and(sub < 2, lane < 128),
            jnp.logical_and(jnp.logical_and(sub >= 2, sub < 4), lane >= 128),
        ),
        1.0,
        0.0,
    ).astype(BF16)
    sub_t = lax.broadcasted_iota(jnp.int32, (16, GROUP), 0)

    @pl.loop(0, n_groups)
    def _(step):
        g = n_groups - 1 - step
        bc, c0, c1, ac = edges(g)
        sq = tot[pl.ds(g, 1), :]
        gd = tot[pl.ds(n_groups + g, 1), :]
        a = 1.0 / jnp.sqrt(sq / width_all + EPSILON)
        c = a * a * (a * gd / width_all)
        a_hi = a.astype(BF16).astype(F32)
        c_hi = c.astype(BF16).astype(F32)
        wide = lambda x: jnp.broadcast_to(x, (16, GROUP))
        terms = jnp.where(
            sub_t == 0,
            wide(a_hi),
            jnp.where(
                sub_t == 1,
                wide(a - a_hi),
                jnp.where(sub_t == 2, wide(c_hi), jnp.where(sub_t == 3, wide(c - c_hi), 0.0)),
            ),
        ).astype(BF16)
        both = dot(terms, spread, 0, 0)
        aa, cc = both[:, :128], both[:, 128:]
        keep = flag(c0 == ac)
        for h in range(n_heads):
            o = o_ref[h, g]
            stage_f[0, g, pl.ds(h, GROUP, stride=n_heads), :] = o * aa
            dob = (heads[GG, h, g].astype(F32) * aa - o * cc).astype(BF16)
            dob_ref[h, g] = dob
            added = dot(heads[QQ, h, g] * gates[GH, g], dob, 0, 0)
            old = r_run[h]
            r_loc[h, g] = old
            r_run[h] = keep * old + added

    scatter(flat(r_run), r_got, r_send, r_recv)

    targets = (out_hbm, dq_hbm, dk_hbm, dv_hbm)

    def store(i, g):
        return pltpu.make_async_copy(stage_b.at[i, g], targets[i].at[g], out_sem.at[i, g])

    def emit(i, g):
        stage_b[i, g] = stage_f[i, g].astype(BF16)
        store(i, g).start()

    def inner_back(g):
        emit(0, g)
        for h in range(n_heads):
            dob = dob_ref[h, g]
            dp = (dot(dob, heads[VV, h, g], 1, 1) * mask_ref[g]).astype(BF16)
            dq = dot(dp, heads[KK, h, g]) + dot(dob * gates[GB, g], s_bf[h, g], 1, 1)
            stage_f[1, g, pl.ds(h, GROUP, stride=n_heads), :] = dq
            dkl_ref[h, g] = dot(dp, heads[QQ, h, g], 0, 0)
            dvl_ref[h, g] = dot(p_ref[h, g], dob, 0, 0)
        emit(1, g)

    @pl.loop(0, half)
    def _(g):
        inner_back(g)

    scatter_done(flat(r_run), r_got, r_send, r_recv)
    combine(flat(r_run), r_got, r_pre, r_in, True)
    give(r_pre, r_in, u_send, u_recv)

    @pl.loop(half, n_groups)
    def _(g):
        inner_back(g)

    give_done(r_pre, r_in, u_send, u_recv)

    @pl.loop(0, n_groups)
    def _(g):
        bc, c0, c1, ac = edges(g)
        w = flag(ac == after_s)
        for h in range(n_heads):
            state = (r_loc[h, g] + w * r_in[h * 128 : h * 128 + 128, :]).astype(BF16)
            stage_f[2, g, pl.ds(h, GROUP, stride=n_heads), :] = dkl_ref[h, g] + dot(
                heads[VV, h, g] * gates[GA, g], state, 1, 1
            )
            stage_f[3, g, pl.ds(h, GROUP, stride=n_heads), :] = dvl_ref[h, g] + dot(
                heads[KK, h, g] * gates[GA, g], state
            )
        emit(2, g)
        emit(3, g)

    @pl.loop(0, n_groups)
    def _(g):
        for i in range(4):
            store(i, g).wait()


def per_device(sizes, queries, keys, values, cotangent, doc_lengths):
    tokens_here, n_heads, width = queries.shape
    n_seq, n_x, n_y = sizes
    n_groups = tokens_here // GROUP
    rows2 = GROUP * n_heads
    slab = n_heads * 128 // n_seq
    view = lambda x: x.reshape(n_groups, rows2, width)
    out = jax.ShapeDtypeStruct((n_groups, rows2, width), BF16)
    dma = pltpu.SemaphoreType.DMA
    vm = pltpu.VMEM
    per_head = (n_heads, n_groups, GROUP, width)
    states = (n_heads, n_groups, width, width)
    exchange = [
        vm((n_heads, width, width), F32),
        vm((n_seq, slab, width), F32),
        vm((n_seq, slab, width), F32),
        vm((n_heads * width, width), F32),
    ]
    sums = (2 * n_groups, GROUP)
    results = pl.pallas_call(
        functools.partial(kernel, (n_seq, n_x, n_y, n_groups, n_heads)),
        out_shape=(out,) * 4,
        in_specs=[pl.BlockSpec(memory_space=pltpu.SMEM)] + [pl.BlockSpec(memory_space=pl.ANY)] * 4,
        out_specs=(pl.BlockSpec(memory_space=pl.ANY),) * 4,
        scratch_shapes=[
            vm((4, n_groups, rows2, width), BF16),
            vm((4, rows2, width), F32),
            vm((4,) + per_head, BF16),
            vm((n_groups, GROUP, GROUP), F32),
            vm((4, n_groups, GROUP, width), BF16),
            vm((n_heads, n_groups, GROUP, GROUP), BF16),
            vm(per_head, F32),
            vm(per_head, BF16),
            vm(per_head, F32),
            vm(per_head, F32),
            vm((4, n_groups, rows2, width), F32),
            vm((4, n_groups, rows2, width), BF16),
            vm(states, F32),
            vm(states, BF16),
            vm(states, F32),
        ]
        + exchange
        + exchange
        + [
            vm(sums, F32),
            vm((n_x,) + sums, F32),
            vm(sums, F32),
            vm((n_y,) + sums, F32),
            vm(sums, F32),
            dma((4, n_groups)),
            dma((4, n_groups)),
        ]
        + [dma((n_seq,))] * 8
        + [dma((n_x,))] * 2
        + [dma((n_y,))] * 2,
        compiler_params=pltpu.CompilerParams(
            collective_id=0, has_side_effects=True, vmem_limit_bytes=64000 * 1024
        ),
    )(doc_lengths, view(queries), view(keys), view(values), view(cotangent))
    return tuple(r.reshape(tokens_here, n_heads, width) for r in results)


def solution(mesh):
    n_x = 4
    spec = P("seq", "head", None)
    return jax.shard_map(
        functools.partial(per_device, (mesh.shape["seq"], n_x, mesh.shape["head"] // n_x)),
        mesh=mesh,
        in_specs=(spec,) * 4 + (P(),),
        out_specs=(spec,) * 4,
        check_vma=False,
    )
```

time: 449 us -> 71.4 us (0.16)
  the two profiles are of different devices: /device:TPU:0 before, /device:TPU:1 now
where the time goes in v1:
time: 71.4 us; the launch traced here: 71.2 us
  Pallas kernels  61.5 us (86%)
  local copies, waits for them, and re-layouts  9.01 us (13%)
    pallas_call x1, Pallas kernels, per_device(): pl.pallas_call(functools.partial(kernel, (n_seq, n_x, n_y, n_groups, n_he...  61.5 us
    unnamed x10, local copies, waits for them, and re-layouts  9.01 us

profile of v1, /device:TPU:1, one launch (start us, length us, event | category | flops | bytes accessed | tf_op | source)
XLA Modules:
  0.0 71.2 jit_solution(15272299965943692871)
XLA Ops:
  0.6 61.5 %shard_map.84 = (bf16[12,512,128]{2,1,0:T(8,128)(2,1)}, bf16[12,512,128]{2,1,0:T(8,128)(2,1)}, bf16[12,512,128]{2,1,0:T(8,128)(2,1)}, bf16[12,512,128]{2,1,0:T(8,128)(2,1)}) custom-call(s32[6]{0:T(128)} %doc_ref.1, bf16[12,512,128]{2,1,0:T(8,128)(2,1)} %bitcast.12, bf16[12,512,128]{2,1,0:T(8,128)(2,1)} %bitcast.13, bf16[12,512,128]{2,1,0:T(8,128)(2,1)} %bitcast.14, ...), custom_call_target="tpu_custom_call" | custom-call | tf_op jit(solution)/shard_map/pallas_call | solution.py:442
  62.2 0.0 copy-start.2
  62.2 3.9 %copy.13 = bf16[3072,2,128]{2,1,0:T(2,128)(2,1)} copy(bf16[3072,2,128]{2,1,0:T(2,128)(2,1)} %bitcast.11) | data formatting | bytes 3145728
  66.1 0.0 copy-done.2
  66.1 0.0 copy-start.1
  66.1 1.1 %copy.14 = bf16[3072,2,128]{2,1,0:T(2,128)(2,1)} copy(bf16[3072,2,128]{2,1,0:T(2,128)(2,1)S(1)} %bitcast.10) | data formatting | bytes 3145728
  67.3 0.8 %copy-done.1 = bf16[12,512,128]{2,1,0:T(8,128)(2,1)S(1)} copy-done((bf16[12,512,128]{2,1,0:T(8,128)(2,1)S(1)}, bf16[12,512,128]{2,1,0:T(8,128)(2,1)}, u32[]{:S(2)}) %copy-start.1) | copy-done | bytes 1572888
  68.1 0.0 copy-start
  68.1 1.1 %copy.15 = bf16[3072,2,128]{2,1,0:T(2,128)(2,1)} copy(bf16[3072,2,128]{2,1,0:T(2,128)(2,1)S(1)} %bitcast.9) | data formatting | bytes 3145728
  69.2 0.8 %copy-done = bf16[12,512,128]{2,1,0:T(8,128)(2,1)S(1)} copy-done((bf16[12,512,128]{2,1,0:T(8,128)(2,1)S(1)}, bf16[12,512,128]{2,1,0:T(8,128)(2,1)}, u32[]{:S(2)}) %copy-start) | copy-done | bytes 1572888
  70.1 1.1 %copy.16 = bf16[3072,2,128]{2,1,0:T(2,128)(2,1)} copy(bf16[3072,2,128]{2,1,0:T(2,128)(2,1)S(1)} %bitcast.8) | data formatting | bytes 3145728
Async XLA Ops:
  62.2 3.9 %copy-start.2 = (bf16[12,512,128]{2,1,0:T(8,128)(2,1)S(1)}, bf16[12,512,128]{2,1,0:T(8,128)(2,1)}, u32[]{:S(2)}) copy-start(bf16[12,512,128]{2,1,0:T(8,128)(2,1)} %get-tuple-element.9) | copy-start | bytes 4718596
  66.1 2.0 %copy-start.1 = (bf16[12,512,128]{2,1,0:T(8,128)(2,1)S(1)}, bf16[12,512,128]{2,1,0:T(8,128)(2,1)}, u32[]{:S(2)}) copy-start(bf16[12,512,128]{2,1,0:T(8,128)(2,1)} %get-tuple-element.10) | copy-start | bytes 4718596
  68.1 2.0 %copy-start = (bf16[12,512,128]{2,1,0:T(8,128)(2,1)S(1)}, bf16[12,512,128]{2,1,0:T(8,128)(2,1)}, u32[]{:S(2)}) copy-start(bf16[12,512,128]{2,1,0:T(8,128)(2,1)} %get-tuple-element.11) | copy-start | bytes 4718596

commit v2 on v1

v2 whole, which is shorter than its diff:
```python
import functools

import jax
import jax.numpy as jnp
from jax import lax
from jax.experimental import pallas as pl
from jax.experimental.pallas import tpu as pltpu
from jax.sharding import PartitionSpec as P

GROUP = 256
EPSILON = 1e-06
CHUNK = 4
MESH = pl.DeviceIdType.MESH
F32 = jnp.float32
BF16 = jnp.bfloat16
KK, VV = range(2)
QQ, GG = range(2)


def dot(a, b, ca=1, cb=0):
    return lax.dot_general(a, b, (((ca,), (cb,)), ((), ())), preferred_element_type=F32)


def flag(cond):
    return jnp.where(cond, 1.0, 0.0).astype(F32)


def doc_ends(doc_ref):
    ends, total = [], 0
    for j in range(doc_ref.shape[0]):
        total = total + doc_ref[j]
        ends.append(total)
    return ends


def seg_of(ends, p):
    s = (ends[0] <= p).astype(jnp.int32)
    for e in ends[1:]:
        s = s + (e <= p).astype(jnp.int32)
    return s


def last_end(ends, p):
    s = jnp.where(ends[0] <= p, ends[0], 0)
    for e in ends[1:]:
        s = jnp.where(e <= p, e, s)
    return s


def next_end(ends, p):
    s = ends[-1]
    for e in ends[-2::-1]:
        s = jnp.where(e > p, e, s)
    return s


def row_gate(lower, limit):
    row = lax.broadcasted_iota(jnp.int32, (GROUP, 128), 0)
    return jnp.where(row >= limit if lower else row < limit, 1.0, 0.0).astype(BF16)


def far_first(n, per_chip):
    chips = n // per_chip

    def hops(d):
        c = d // per_chip
        return min(c, chips - c)

    return sorted(range(1, n), key=lambda d: -hops(d))


def main_kernel(
    sizes,
    doc_ref,
    q_hbm,
    k_hbm,
    v_hbm,
    g_hbm,
    out_v,
    dq_v,
    dkl_ref,
    dvl_ref,
    kv,
    r_loc,
    r_in,
    raw,
    tmp,
    qg,
    mask_ref,
    p_ref,
    o_ref,
    dob_ref,
    stage,
    s_loc,
    s_bf,
    keep_ref,
    s_run,
    s_got,
    s_pre,
    s_in,
    r_run,
    r_got,
    r_pre,
    part,
    t_got,
    tot,
    in_sem,
    s_send,
    s_recv,
    t_send,
    t_recv,
    r_send,
    r_recv,
    u_send,
    u_recv,
    a_send,
    a_recv,
):
    n_seq, n_x, n_y, n_groups, n_heads = sizes
    tokens = n_groups * GROUP
    n_head = n_x * n_y
    width_all = float(n_head * n_heads * 128)
    n_chunks = n_groups // CHUNK
    me = lax.axis_index("seq")
    head = lax.axis_index("head")
    mx = lax.rem(head, n_x)
    my = head // n_x
    slab = 128 // n_seq
    seq_order = far_first(n_seq, 2)
    head_order = sorted(
        range(1, n_head),
        key=lambda d: -(min(d % n_x, n_x - d % n_x) + min(d // n_x, n_y - d // n_x)),
    )

    def seq_peer(d):
        return lax.rem(me + d, n_seq)

    def head_peer(d, sign):
        x = lax.rem(mx + n_x + sign * (d % n_x), n_x)
        y = lax.rem(my + n_y + sign * (d // n_x), n_y)
        return y * n_x + x

    barrier = pltpu.get_barrier_semaphore()
    for d in seq_order:
        pl.semaphore_signal(barrier, inc=1, device_id={"seq": seq_peer(d)}, device_id_type=MESH)
    for d in head_order:
        pl.semaphore_signal(barrier, inc=1, device_id={"head": head_peer(d, 1)}, device_id_type=MESH)

    sources = (k_hbm, v_hbm, q_hbm, g_hbm)

    def load(a, g):
        return pltpu.make_async_copy(sources[a].at[g], raw.at[a, g], in_sem.at[a, g])

    @pl.loop(0, n_groups)
    def _(g):
        load(0, g).start()
        load(1, g).start()

    @pl.loop(0, n_groups)
    def _(g):
        load(2, g).start()
        load(3, g).start()

    ends = doc_ends(doc_ref)
    shard_first = me * tokens
    bs = seg_of(ends, shard_first - 1)

    def edges(g):
        first = shard_first + g * GROUP
        return (
            seg_of(ends, first - 1),
            seg_of(ends, first),
            seg_of(ends, first + GROUP - 1),
            seg_of(ends, first + GROUP),
        )

    def before_gate(g):
        first = shard_first + g * GROUP
        return row_gate(False, next_end(ends, first - 1) - first)

    def tail_gate(g):
        first = shard_first + g * GROUP
        return row_gate(True, last_end(ends, first + GROUP - 1) - first)

    def lead_gate(g):
        first = shard_first + g * GROUP
        return row_gate(False, next_end(ends, first) - first)

    for i in range(n_seq):
        first = i * tokens
        keep_ref[0, i] = flag(seg_of(ends, first + tokens - 1) == seg_of(ends, first - 1))
        keep_ref[1, i] = flag(seg_of(ends, first) == seg_of(ends, first + tokens))

    def split(a, g, into, i):
        tmp[a] = raw[a, g].astype(F32)
        for h in range(n_heads):
            into[i, h, g] = tmp[a, pl.ds(h, GROUP, stride=n_heads), :].astype(BF16)

    def key_state(g, h):
        bc, c0, c1, ac = edges(g)
        added = dot(kv[KK, h, g] * tail_gate(g), kv[VV, h, g], 0, 0)
        old = s_run[h]
        s_loc[h, g] = old
        s_run[h] = flag(c1 == bc) * old + added

    def hand(src, dst, send, recv, d):
        return pltpu.make_async_remote_copy(
            src_ref=src,
            dst_ref=dst,
            send_sem=send.at[d],
            recv_sem=recv.at[me],
            device_id={"seq": seq_peer(d)},
            device_id_type=MESH,
        )

    def taken(dst, send, recv, d):
        return pltpu.make_async_remote_copy(
            src_ref=dst,
            dst_ref=dst,
            send_sem=send.at[d],
            recv_sem=recv.at[seq_peer(d)],
            device_id={"seq": seq_peer(d)},
            device_id_type=MESH,
        )

    def rows(ref, h, i):
        return ref.at[h, pl.ds(pl.multiple_of(i * slab, slab), slab)]

    def scatter(h, run, got, send, recv):
        for d in seq_order:
            hand(rows(run, h, seq_peer(d)), got.at[h, me], send.at[h], recv.at[h], d).start()

    def combine(h, run, got, pre, into, send, recv, backward):
        mine = pl.ds(pl.multiple_of(me * slab, slab), slab)
        got[h, me] = run[h, mine, :]
        for d in reversed(seq_order):
            taken(got.at[h, seq_peer(d)], send.at[h], recv.at[h], d).wait_recv()
        carry = jnp.zeros((slab, 128), F32)
        for i in range(n_seq - 1, -1, -1) if backward else range(n_seq):
            pre[h, i] = carry
            carry = keep_ref[1 if backward else 0, i] * carry + got[h, i]
        into[h, mine, :] = pre[h, me]

    def give(h, pre, into, send, recv):
        for d in seq_order:
            hand(pre.at[h, seq_peer(d)], rows(into, h, me), send.at[h], recv.at[h], d).start()

    def give_done(h, into, send, recv):
        for d in reversed(seq_order):
            taken(rows(into, h, seq_peer(d)), send.at[h], recv.at[h], d).wait_recv()

    def sends_done(h, run, got, send, recv, pre, into, send2, recv2):
        for d in seq_order:
            hand(rows(run, h, seq_peer(d)), got.at[h, me], send.at[h], recv.at[h], d).wait_send()
            hand(pre.at[h, seq_peer(d)], rows(into, h, me), send2.at[h], recv2.at[h], d).wait_send()

    s_run[...] = jnp.zeros_like(s_run)
    part[...] = jnp.zeros_like(part)

    @pl.loop(0, n_groups)
    def _(g):
        load(0, g).wait()
        load(1, g).wait()
        split(0, g, kv, KK)
        split(1, g, kv, VV)
        key_state(g, 0)

    pl.semaphore_wait(barrier, n_seq - 1 + n_head - 1)
    scatter(0, s_run, s_got, s_send, s_recv)

    for h in range(1, n_heads):

        @pl.loop(0, n_groups)
        def _(g):
            key_state(g, h)

        scatter(h, s_run, s_got, s_send, s_recv)

    @pl.loop(0, n_groups)
    def _(g):
        first = shard_first + g * GROUP
        row = lax.broadcasted_iota(jnp.int32, (GROUP, 128), 0)
        start = last_end(ends, row + first) - first
        for half in range(2):
            lane = lax.broadcasted_iota(jnp.int32, (GROUP, 128), 1) + half * 128
            mask_ref[g, :, half * 128 : half * 128 + 128] = jnp.where(
                jnp.logical_and(lane >= start, row >= lane), 1.0, 0.0
            ).astype(F32)

    def intra(g):
        load(2, g).wait()
        split(2, g, qg, QQ)
        for h in range(n_heads):
            scores = dot(qg[QQ, h, g], kv[KK, h, g], 1, 1)
            probs = (scores * mask_ref[g]).astype(BF16)
            p_ref[h, g] = probs
            o_ref[h, g] = dot(probs, kv[VV, h, g])

    cut1, cut2 = (2 * n_groups) // 3, (5 * n_groups) // 6

    @pl.loop(0, cut1)
    def _(g):
        intra(g)

    combine(0, s_run, s_got, s_pre, s_in, s_send, s_recv, False)
    give(0, s_pre, s_in, t_send, t_recv)

    @pl.loop(cut1, cut2)
    def _(g):
        intra(g)

    for h in range(1, n_heads):
        combine(h, s_run, s_got, s_pre, s_in, s_send, s_recv, False)
        give(h, s_pre, s_in, t_send, t_recv)

    @pl.loop(cut2, n_groups)
    def _(g):
        intra(g)

    @pl.loop(0, n_groups)
    def _(g):
        load(3, g).wait()
        split(3, g, qg, GG)

    ones = jnp.ones((16, 128), BF16)

    def outer(g, h):
        bc, c0, c1, ac = edges(g)
        w = flag(bc == bs)
        state = (s_loc[h, g] + w * s_in[h]).astype(BF16)
        s_bf[h, g] = state
        o = o_ref[h, g] + dot(qg[QQ, h, g] * before_gate(g), state)
        o_ref[h, g] = o
        c, r = g // CHUNK, lax.rem(g, CHUNK)
        squares = dot(ones, (o * o).astype(BF16), 1, 1)[0:1]
        inner = dot(ones, (qg[GG, h, g].astype(F32) * o).astype(BF16), 1, 1)[0:1]
        part[c, pl.ds(r, 1), :] += squares
        part[c, pl.ds(CHUNK + r, 1), :] += inner

    for h in range(n_heads - 1):
        give_done(h, s_in, t_send, t_recv)

        @pl.loop(0, n_groups)
        def _(g):
            outer(g, h)

    give_done(n_heads - 1, s_in, t_send, t_recv)

    def part_copy(c, d, wait):
        slot = head_peer(d, 1) if wait else head
        return pltpu.make_async_remote_copy(
            src_ref=part.at[c],
            dst_ref=t_got.at[c, slot],
            send_sem=a_send.at[c, d],
            recv_sem=a_recv.at[c, slot],
            device_id={"head": head_peer(d, 1)},
            device_id_type=MESH,
        )

    for c in range(n_chunks - 1, -1, -1):

        @pl.loop(0, CHUNK)
        def _(r):
            outer(c * CHUNK + r, n_heads - 1)

        for d in head_order:
            part_copy(c, d, False).start()
        t_got[c, head] = part[c]

    r_run[...] = jnp.zeros_like(r_run)
    sub = lax.broadcasted_iota(jnp.int32, (16, 256), 0)
    lane = lax.broadcasted_iota(jnp.int32, (16, 256), 1)
    spread = jnp.where(
        jnp.logical_or(
            jnp.logical_and(sub < 2, lane < 128),
            jnp.logical_and(jnp.logical_and(sub >= 2, sub < 4), lane >= 128),
        ),
        1.0,
        0.0,
    ).astype(BF16)
    sub_t = lax.broadcasted_iota(jnp.int32, (16, GROUP), 0)

    def scales(g):
        c, r = g // CHUNK, lax.rem(g, CHUNK)
        sq = tot[c, pl.ds(r, 1), :]
        gd = tot[c, pl.ds(CHUNK + r, 1), :]
        a = 1.0 / jnp.sqrt(sq / width_all + EPSILON)
        b = a * a * (a * gd / width_all)
        a_hi = a.astype(BF16).astype(F32)
        b_hi = b.astype(BF16).astype(F32)
        wide = lambda x: jnp.broadcast_to(x, (16, GROUP))
        terms = jnp.where(
            sub_t == 0,
            wide(a_hi),
            jnp.where(
                sub_t == 1,
                wide(a - a_hi),
                jnp.where(sub_t == 2, wide(b_hi), jnp.where(sub_t == 3, wide(b - b_hi), 0.0)),
            ),
        ).astype(BF16)
        both = dot(terms, spread, 0, 0)
        return both[:, :128], both[:, 128:]

    def back_state(g, aa, bb, h):
        bc, c0, c1, ac = edges(g)
        dob = (qg[GG, h, g].astype(F32) * aa - o_ref[h, g] * bb).astype(BF16)
        dob_ref[h, g] = dob
        added = dot(qg[QQ, h, g] * lead_gate(g), dob, 0, 0)
        old = r_run[h]
        r_loc[h, g] = old
        r_run[h] = flag(c0 == ac) * old + added

    def gather_part(c):
        for d in reversed(head_order):
            part_copy(c, d, True).wait_recv()
        value = t_got[c, 0]
        for i in range(1, n_head):
            value = value + t_got[c, i]
        tot[c] = value

    for c in range(n_chunks - 1, 0, -1):
        gather_part(c)

        @pl.loop(0, CHUNK)
        def _(step):
            g = c * CHUNK + CHUNK - 1 - step
            aa, bb = scales(g)
            for h in range(n_heads):
                back_state(g, aa, bb, h)

    gather_part(0)
    for h in range(n_heads):

        @pl.loop(0, CHUNK)
        def _(step):
            g = CHUNK - 1 - step
            aa, bb = scales(g)
            back_state(g, aa, bb, h)

        scatter(h, r_run, r_got, r_send, r_recv)

    def inner_back(g):
        aa, _ = scales(g)
        before = before_gate(g)
        for h in range(n_heads):
            even = pl.ds(h, GROUP, stride=n_heads)
            stage[0, even, :] = o_ref[h, g] * aa
            dob = dob_ref[h, g]
            dp = (dot(dob, kv[VV, h, g], 1, 1) * mask_ref[g]).astype(BF16)
            dq = dot(dp, kv[KK, h, g]) + dot(dob * before, s_bf[h, g], 1, 1)
            stage[1, even, :] = dq
            dkl_ref[h, g] = dot(dp, qg[QQ, h, g], 0, 0)
            dvl_ref[h, g] = dot(p_ref[h, g], dob, 0, 0)
        out_v[g] = stage[0].astype(BF16)
        dq_v[g] = stage[1].astype(BF16)

    cut1, cut2 = (2 * n_groups) // 3, (5 * n_groups) // 6

    @pl.loop(0, cut1)
    def _(g):
        inner_back(g)

    combine(0, r_run, r_got, r_pre, r_in, r_send, r_recv, True)
    give(0, r_pre, r_in, u_send, u_recv)

    @pl.loop(cut1, cut2)
    def _(g):
        inner_back(g)

    for h in range(1, n_heads):
        combine(h, r_run, r_got, r_pre, r_in, r_send, r_recv, True)
        give(h, r_pre, r_in, u_send, u_recv)

    @pl.loop(cut2, n_groups)
    def _(g):
        inner_back(g)

    for h in range(n_heads):
        sends_done(h, s_run, s_got, s_send, s_recv, s_pre, s_in, t_send, t_recv)
    for c in range(n_chunks):
        for d in head_order:
            part_copy(c, d, False).wait_send()
    for h in range(n_heads):
        give_done(h, r_in, u_send, u_recv)
        sends_done(h, r_run, r_got, r_send, r_recv, r_pre, r_in, u_send, u_recv)


def last_kernel(
    sizes,
    doc_ref,
    out_v,
    dq_v,
    dkl_ref,
    dvl_ref,
    kv,
    r_loc,
    r_in,
    out_hbm,
    dq_hbm,
    dk_hbm,
    dv_hbm,
    stage,
    done,
    sem,
    whole,
):
    n_seq, n_x, n_y, n_groups, n_heads = sizes
    tokens = n_groups * GROUP
    shard_first = lax.axis_index("seq") * tokens
    copies = [
        pltpu.make_async_copy(out_v, out_hbm, whole.at[0]),
        pltpu.make_async_copy(dq_v, dq_hbm, whole.at[1]),
    ]
    for c in copies:
        c.start()
    ends = doc_ends(doc_ref)
    after_s = seg_of(ends, shard_first + tokens)
    targets = (dk_hbm, dv_hbm)

    def store(i, g):
        return pltpu.make_async_copy(done.at[i, g], targets[i].at[g], sem.at[i, g])

    @pl.loop(0, n_groups)
    def _(g):
        first = shard_first + g * GROUP
        w = flag(seg_of(ends, first + GROUP) == after_s)
        after = row_gate(True, last_end(ends, first + GROUP) - first)
        for h in range(n_heads):
            even = pl.ds(h, GROUP, stride=n_heads)
            state = (r_loc[h, g] + w * r_in[h]).astype(BF16)
            stage[0, even, :] = dkl_ref[h, g] + dot(kv[VV, h, g] * after, state, 1, 1)
            stage[1, even, :] = dvl_ref[h, g] + dot(kv[KK, h, g] * after, state)
        for i in range(2):
            done[i, g] = stage[i].astype(BF16)
            store(i, g).start()

    @pl.loop(0, n_groups)
    def _(g):
        for i in range(2):
            store(i, g).wait()

    for c in copies:
        c.wait()


def per_device(sizes, queries, keys, values, cotangent, doc_lengths):
    tokens_here, n_heads, width = queries.shape
    n_seq, n_x, n_y = sizes
    n_groups = tokens_here // GROUP
    n_chunks = n_groups // CHUNK
    rows2 = GROUP * n_heads
    slab = width // n_seq
    sizes = (n_seq, n_x, n_y, n_groups, n_heads)
    view = lambda x: x.reshape(n_groups, rows2, width)
    dma = pltpu.SemaphoreType.DMA
    vm = pltpu.VMEM
    anywhere = pl.BlockSpec(memory_space=pl.ANY)
    on_chip = pl.BlockSpec(memory_space=pltpu.VMEM)
    scalars = pl.BlockSpec(memory_space=pltpu.SMEM)
    per_head = (n_heads, n_groups, GROUP, width)
    states = (n_heads, n_groups, width, width)
    one_state = (n_heads, width, width)
    slices = (n_heads, n_seq, slab, width)
    sums = (n_chunks, 2 * CHUNK, GROUP)
    packed = (n_groups, rows2, width)
    mids = pl.pallas_call(
        functools.partial(main_kernel, sizes),
        out_shape=(
            vm(packed, BF16),
            vm(packed, BF16),
            vm(per_head, F32),
            vm(per_head, F32),
            vm((2,) + per_head, BF16),
            vm(states, F32),
            vm(one_state, F32),
        ),
        in_specs=[scalars] + [anywhere] * 4,
        out_specs=(on_chip,) * 7,
        scratch_shapes=[
            vm((4,) + packed, BF16),
            vm((4, rows2, width), F32),
            vm((2,) + per_head, BF16),
            vm((n_groups, GROUP, GROUP), F32),
            vm((n_heads, n_groups, GROUP, GROUP), BF16),
            vm(per_head, F32),
            vm(per_head, BF16),
            vm((2, rows2, width), F32),
            vm(states, F32),
            vm(states, BF16),
            pltpu.SMEM((2, n_seq), F32),
            vm(one_state, F32),
            vm(slices, F32),
            vm(slices, F32),
            vm(one_state, F32),
            vm(one_state, F32),
            vm(slices, F32),
            vm(slices, F32),
            vm(sums, F32),
            vm((n_chunks, n_x * n_y, 2 * CHUNK, GROUP), F32),
            vm(sums, F32),
            dma((4, n_groups)),
        ]
        + [dma((n_heads, n_seq))] * 8
        + [dma((n_chunks, n_x * n_y))] * 2,
        compiler_params=pltpu.CompilerParams(
            collective_id=0, has_side_effects=True, vmem_limit_bytes=44 << 20
        ),
        name="exchange_and_attend",
    )(doc_lengths, view(queries), view(keys), view(values), view(cotangent))
    mids = [pltpu.with_memory_space_constraint(m, pltpu.VMEM) for m in mids]
    results = pl.pallas_call(
        functools.partial(last_kernel, sizes),
        out_shape=(jax.ShapeDtypeStruct(packed, BF16),) * 4,
        in_specs=[scalars] + [on_chip] * 7,
        out_specs=(anywhere,) * 4,
        scratch_shapes=[
            vm((2, rows2, width), F32),
            vm((2,) + packed, BF16),
            dma((2, n_groups)),
            dma((2,)),
        ],
        compiler_params=pltpu.CompilerParams(vmem_limit_bytes=16 << 20),
        name="finish",
    )(doc_lengths, *mids)
    return tuple(r.reshape(tokens_here, n_heads, width) for r in results)


def solution(mesh):
    n_x = 4
    spec = P("seq", "head", None)
    return jax.shard_map(
        functools.partial(per_device, (mesh.shape["seq"], n_x, mesh.shape["head"] // n_x)),
        mesh=mesh,
        in_specs=(spec,) * 4 + (P(),),
        out_specs=(spec,) * 4,
        check_vma=False,
    )
```

time: 71.4 us -> 65.3 us (0.915)
  local copies, waits for them, and re-layouts: 9.01 us -> 0.01 us
  Pallas kernels: 61.5 us -> 64.5 us
    unnamed x10 -> x2, local copies, waits for them, and re-layouts: 9.01 us -> 0.01 us
    pallas_call x1 -> x2, Pallas kernels: 61.5 us -> 64.5 us  [the longest x1 59.9 us: per_device(): pl.pallas_call(functools.partial(main_kernel, sizes), out_shape=(vm(packe...]
where the time goes in v2:
time: 65.3 us; the launch traced here: 65.2 us
  Pallas kernels  64.5 us (99%)
  between operations  0.66 us (1%)
    pallas_call x1, Pallas kernels, per_device(): pl.pallas_call(functools.partial(main_kernel, sizes), out_shape=(vm(packe...  59.9 us
    pallas_call x1, Pallas kernels, per_device(): pl.pallas_call(functools.partial(last_kernel, sizes), out_shape=(jax.Shap...  4.61 us

profile of v2, /device:TPU:1, one launch (start us, length us, event | category | flops | bytes accessed | tf_op | source)
XLA Modules:
  0.0 65.2 jit_solution(6713427044821024669)
XLA Ops:
  0.6 0.0 copy-start
  0.6 59.9 %exchange_and_attend.1 = (bf16[12,512,128]{2,1,0:T(8,128)(2,1)S(1)}, bf16[12,512,128]{2,1,0:T(8,128)(2,1)S(1)}, f32[2,12,256,128]{3,2,1,0:T(8,128)S(1)}, f32[2,1...) custom-call(s32[6]{0:T(128)} %doc_ref.3, ...), custom_call_target="tpu_custom_call" | custom-call | tf_op jit(solution)/shard_map/exchange_and_attend/pallas_call | solution.py:566
  60.6 0.0 copy-done
  60.6 4.6 %finish.1 = (bf16[12,512,128]{2,1,0:T(8,128)(2,1)}, bf16[12,512,128]{2,1,0:T(8,128)(2,1)}, bf16[12,512,128]{2,1,0:T(8,128)(2,1)}, bf16[12,512,128]{2,1,0:T(8,128)(2,1)}) custom-call(s32[6]{0:T(128)S(1)} %copy-done, bf16[12,512,128]{2,1,0:T(8,128)(2,1)S(1)} %get-tuple-element.15.out_v, bf16[12,512,128]{2,1,0:T(8,128)(2,1)S(1)} %get-tuple-element.16.dq_v, ...), custom_call_target="tpu_custom_call" | custom-call | tf_op jit(solution)/shard_map/finish/pallas_call | solution.py:611
Async XLA Ops:
  0.6 60.0 %copy-start = (s32[6]{0:T(128)S(1)}, s32[6]{0:T(128)}, u32[]{:S(2)}) copy-start(s32[6]{0:T(128)} %doc_ref.3) | copy-start | bytes 76

commit v3 on v2

v3 whole, which is shorter than its diff:
```python
import functools

import jax
import jax.numpy as jnp
from jax import lax
from jax.experimental import pallas as pl
from jax.experimental.pallas import tpu as pltpu
from jax.sharding import PartitionSpec as P

GROUP = 256
EPSILON = 1e-06
CHUNK = 4
MESH = pl.DeviceIdType.MESH
F32 = jnp.float32
BF16 = jnp.bfloat16
KK, VV = range(2)
QQ, GG = range(2)


def dot(a, b, ca=1, cb=0):
    return lax.dot_general(a, b, (((ca,), (cb,)), ((), ())), preferred_element_type=F32)


def flag(cond):
    return jnp.where(cond, 1.0, 0.0).astype(F32)


def doc_ends(doc_ref):
    ends, total = [], 0
    for j in range(doc_ref.shape[0]):
        total = total + doc_ref[j]
        ends.append(total)
    return ends


def seg_of(ends, p):
    s = (ends[0] <= p).astype(jnp.int32)
    for e in ends[1:]:
        s = s + (e <= p).astype(jnp.int32)
    return s


def last_end(ends, p):
    s = jnp.where(ends[0] <= p, ends[0], 0)
    for e in ends[1:]:
        s = jnp.where(e <= p, e, s)
    return s


def next_end(ends, p):
    s = ends[-1]
    for e in ends[-2::-1]:
        s = jnp.where(e > p, e, s)
    return s


def lane_gate(lower, limit):
    lane = lax.broadcasted_iota(jnp.int32, (16, GROUP), 1)
    one = jnp.where(lane >= limit if lower else lane < limit, 1.0, 0.0).astype(BF16)
    return jnp.concatenate([one] * 8, axis=0)


def far_first(n, per_chip):
    chips = n // per_chip

    def hops(d):
        c = d // per_chip
        return min(c, chips - c)

    return sorted(range(1, n), key=lambda d: -hops(d))


def main_kernel(
    sizes,
    doc_ref,
    q_hbm,
    k_hbm,
    v_hbm,
    g_hbm,
    out_v,
    dq_v,
    dk_t,
    dv_t,
    k_t,
    v_t,
    r_loc,
    r_in,
    raw,
    tmp,
    k_n,
    v_n,
    q_t,
    g_t,
    mask_ref,
    p_t,
    dp_t,
    o_t,
    dob_t,
    stage,
    s_loc,
    s_bf,
    keep_ref,
    s_got,
    s_pre,
    s_in,
    r_got,
    r_pre,
    part,
    t_got,
    scale_a,
    scale_b,
    in_sem,
    s_send,
    s_recv,
    t_send,
    t_recv,
    r_send,
    r_recv,
    u_send,
    u_recv,
    a_send,
    a_recv,
):
    n_seq, n_x, n_y, n_groups, n_heads = sizes
    tokens = n_groups * GROUP
    n_head = n_x * n_y
    width_all = float(n_head * n_heads * 128)
    n_chunks = n_groups // CHUNK
    me = lax.axis_index("seq")
    head = lax.axis_index("head")
    mx = lax.rem(head, n_x)
    my = head // n_x
    slab = 128 // n_seq
    seq_order = far_first(n_seq, 2)
    head_order = sorted(
        range(1, n_head),
        key=lambda d: -(min(d % n_x, n_x - d % n_x) + min(d // n_x, n_y - d // n_x)),
    )

    def seq_peer(d):
        return lax.rem(me + d, n_seq)

    def head_peer(d, sign):
        x = lax.rem(mx + n_x + sign * (d % n_x), n_x)
        y = lax.rem(my + n_y + sign * (d // n_x), n_y)
        return y * n_x + x

    sources = (k_hbm, v_hbm, q_hbm, g_hbm)

    def load(a, g):
        return pltpu.make_async_copy(sources[a].at[g], raw.at[a, g], in_sem.at[a, g])

    @pl.loop(0, n_groups)
    def _(g):
        load(0, g).start()
        load(1, g).start()

    @pl.loop(0, n_groups)
    def _(g):
        load(2, g).start()
        load(3, g).start()

    barrier = pltpu.get_barrier_semaphore()
    for d in seq_order:
        pl.semaphore_signal(barrier, inc=1, device_id={"seq": seq_peer(d)}, device_id_type=MESH)
    for d in head_order:
        pl.semaphore_signal(barrier, inc=1, device_id={"head": head_peer(d, 1)}, device_id_type=MESH)

    ends = doc_ends(doc_ref)
    shard_first = me * tokens
    bs = seg_of(ends, shard_first - 1)

    def edges(g):
        first = shard_first + g * GROUP
        return (
            seg_of(ends, first - 1),
            seg_of(ends, first),
            seg_of(ends, first + GROUP - 1),
            seg_of(ends, first + GROUP),
        )

    def before_gate(g):
        first = shard_first + g * GROUP
        return lane_gate(False, next_end(ends, first - 1) - first)

    def tail_gate(g):
        first = shard_first + g * GROUP
        return lane_gate(True, last_end(ends, first + GROUP - 1) - first)

    def lead_gate(g):
        first = shard_first + g * GROUP
        return lane_gate(False, next_end(ends, first) - first)

    both_heads = range(n_heads)

    def spread(a, g, slot):
        tmp[slot] = raw[a, g].astype(F32)
        return [tmp[slot, pl.ds(h, GROUP, stride=n_heads), :].astype(BF16) for h in both_heads]

    def join(slot, parts):
        for h in both_heads:
            stage[slot, pl.ds(h, GROUP, stride=n_heads), :] = parts[h].astype(BF16).T.astype(F32)
        return stage[slot].astype(BF16)

    def key_states(groups, h):
        added = [dot(v_t[h, g] * tail_gate(g), k_n[h, g]) for g in groups]
        for g, new in zip(groups, added):
            bc, c0, c1, ac = edges(g)
            s_loc[h, g + 1] = flag(c1 == bc) * s_loc[h, g] + new

    def hand(src, dst, send, recv, d):
        return pltpu.make_async_remote_copy(
            src_ref=src,
            dst_ref=dst,
            send_sem=send.at[d],
            recv_sem=recv.at[me],
            device_id={"seq": seq_peer(d)},
            device_id_type=MESH,
        )

    def taken(dst, send, recv, d):
        return pltpu.make_async_remote_copy(
            src_ref=dst,
            dst_ref=dst,
            send_sem=send.at[d],
            recv_sem=recv.at[seq_peer(d)],
            device_id={"seq": seq_peer(d)},
            device_id_type=MESH,
        )

    def rows(ref, h, i):
        return ref.at[h, pl.ds(pl.multiple_of(i * slab, slab), slab)]

    class Run:
        def __init__(self, ref, slot):
            self.ref, self.slot = ref, slot

        @property
        def at(self):
            return self

        def __getitem__(self, index):
            h, rest = index
            return self.ref.at[h, self.slot, rest]

    s_run, r_run = Run(s_loc, n_groups), Run(r_loc, 0)

    def scatter(h, run, got, send, recv):
        for d in seq_order:
            hand(rows(run, h, seq_peer(d)), got.at[h, me], send.at[h], recv.at[h], d).start()

    def combine(h, run, got, pre, into, send, recv, backward):
        mine = pl.ds(pl.multiple_of(me * slab, slab), slab)
        got[h, me] = run.ref[h, run.slot, mine, :]
        for d in reversed(seq_order):
            taken(got.at[h, seq_peer(d)], send.at[h], recv.at[h], d).wait_recv()
        carry = jnp.zeros((slab, 128), F32)
        for i in range(n_seq - 1, -1, -1) if backward else range(n_seq):
            pre[h, i] = carry
            carry = keep_ref[1 if backward else 0, i] * carry + got[h, i]
        into[h, mine, :] = pre[h, me]

    def give(h, pre, into, send, recv):
        for d in seq_order:
            hand(pre.at[h, seq_peer(d)], rows(into, h, me), send.at[h], recv.at[h], d).start()

    def give_done(h, into, send, recv):
        for d in reversed(seq_order):
            taken(rows(into, h, seq_peer(d)), send.at[h], recv.at[h], d).wait_recv()

    def sends_done(h, run, got, send, recv, pre, into, send2, recv2):
        for d in seq_order:
            hand(rows(run, h, seq_peer(d)), got.at[h, me], send.at[h], recv.at[h], d).wait_send()
            hand(pre.at[h, seq_peer(d)], rows(into, h, me), send2.at[h], recv2.at[h], d).wait_send()

    pair = 2
    for h in both_heads:
        s_loc[h, 0] = jnp.zeros((128, 128), F32)

    @pl.loop(0, n_groups // pair)
    def _(i):
        groups = [i * pair + u for u in range(pair)]
        for g in groups:
            load(0, g).wait()
            load(1, g).wait()
        for u, g in enumerate(groups):
            for h, x in enumerate(spread(0, g, 2 * u)):
                k_n[h, g] = x
            for h, x in enumerate(spread(1, g, 2 * u + 1)):
                v_n[h, g] = x
                v_t[h, g] = x.T
        key_states(groups, 0)

    pl.semaphore_wait(barrier, n_seq - 1 + n_head - 1)
    scatter(0, s_run, s_got, s_send, s_recv)

    for h in range(1, n_heads):

        @pl.loop(0, n_groups // CHUNK)
        def _(i):
            key_states([i * CHUNK + u for u in range(CHUNK)], h)

        scatter(h, s_run, s_got, s_send, s_recv)

    for i in range(n_seq):
        first = i * tokens
        keep_ref[0, i] = flag(seg_of(ends, first + tokens - 1) == seg_of(ends, first - 1))
        keep_ref[1, i] = flag(seg_of(ends, first) == seg_of(ends, first + tokens))

    def build_mask(g):
        first = shard_first + g * GROUP
        lane8 = lax.broadcasted_iota(jnp.int32, (8, GROUP), 1)
        start = jnp.broadcast_to((last_end(ends, lane8 + first) - first)[0:1], (GROUP, GROUP))
        key = lax.broadcasted_iota(jnp.int32, (GROUP, GROUP), 0)
        query = lax.broadcasted_iota(jnp.int32, (GROUP, GROUP), 1)
        mask_ref[g] = jnp.where(jnp.logical_and(key >= start, key <= query), 1.0, 0.0).astype(F32)

    def intra(i):
        groups = [i * pair + u for u in range(pair)]
        for u, g in enumerate(groups):
            load(2, g).wait()
            build_mask(g)
            for h, x in enumerate(spread(2, g, u)):
                q_t[h, g] = x.T
                k_t[h, g] = k_n[h, g].T
        for g in groups:
            for h in both_heads:
                p_t[h, g] = (dot(k_n[h, g], q_t[h, g]) * mask_ref[g]).astype(BF16)
        for g in groups:
            for h in both_heads:
                o_t[h, g] = dot(v_t[h, g], p_t[h, g])

    n_pairs = n_groups // pair
    cut1, cut2 = (2 * n_pairs) // 3, (5 * n_pairs) // 6

    @pl.loop(0, cut1)
    def _(i):
        intra(i)

    combine(0, s_run, s_got, s_pre, s_in, s_send, s_recv, False)
    give(0, s_pre, s_in, t_send, t_recv)

    @pl.loop(cut1, cut2)
    def _(i):
        intra(i)

    for h in range(1, n_heads):
        combine(h, s_run, s_got, s_pre, s_in, s_send, s_recv, False)
        give(h, s_pre, s_in, t_send, t_recv)

    @pl.loop(cut2, n_pairs)
    def _(i):
        intra(i)

    @pl.loop(0, n_pairs)
    def _(i):
        groups = [i * pair + u for u in range(pair)]
        for u, g in enumerate(groups):
            load(3, g).wait()
            for h, x in enumerate(spread(3, g, u)):
                g_t[h, g] = x.T

    def outer(groups, h):
        for g in groups:
            bc, c0, c1, ac = edges(g)
            s_bf[h, g] = (s_loc[h, g] + flag(bc == bs) * s_in[h]).astype(BF16)
        more = [dot(s_bf[h, g], q_t[h, g] * before_gate(g)) for g in groups]
        for g, x in zip(groups, more):
            o = o_t[h, g] + x
            o_t[h, g] = o
            c, r = g // CHUNK, lax.rem(g, CHUNK)
            squares = jnp.sum(o * o, axis=0, keepdims=True)
            inner = jnp.sum(g_t[h, g].astype(F32) * o, axis=0, keepdims=True)
            one, two = pl.ds(r, 1), pl.ds(CHUNK + r, 1)
            if h == 0:
                part[c, one, :] = squares
                part[c, two, :] = inner
            else:
                part[c, one, :] += squares
                part[c, two, :] += inner

    for h in range(n_heads - 1):
        give_done(h, s_in, t_send, t_recv)

        @pl.loop(0, n_pairs)
        def _(i):
            outer([i * pair + u for u in range(pair)], h)

    give_done(n_heads - 1, s_in, t_send, t_recv)

    def part_copy(c, d, wait):
        slot = head_peer(d, 1) if wait else head
        return pltpu.make_async_remote_copy(
            src_ref=part.at[c],
            dst_ref=t_got.at[c, slot],
            send_sem=a_send.at[c, d],
            recv_sem=a_recv.at[c, slot],
            device_id={"head": head_peer(d, 1)},
            device_id_type=MESH,
        )

    for c in range(n_chunks - 1, -1, -1):

        @pl.loop(0, CHUNK // pair)
        def _(i):
            outer([c * CHUNK + i * pair + u for u in range(pair)], n_heads - 1)

        for d in head_order:
            part_copy(c, d, False).start()
        t_got[c, head] = part[c]

    for h in both_heads:
        r_loc[h, n_groups] = jnp.zeros((128, 128), F32)

    def wide(ref, g):
        c, r = g // CHUNK, lax.rem(g, CHUNK)
        return jnp.broadcast_to(ref[c, pl.ds(r, 1), :], (128, GROUP))

    def back_states(groups, heads):
        for g in groups:
            for h in heads:
                dob_t[h, g] = (g_t[h, g].astype(F32) * wide(scale_a, g) - o_t[h, g] * wide(scale_b, g)).astype(BF16)
        added = [[dot(q_t[h, g] * lead_gate(g), dob_t[h, g], 1, 1) for h in heads] for g in groups]
        for g, row in zip(groups, added):
            bc, c0, c1, ac = edges(g)
            for h, new in zip(heads, row):
                r_loc[h, g] = flag(c0 == ac) * r_loc[h, g + 1] + new

    def gather_part(c):
        for d in reversed(head_order):
            part_copy(c, d, True).wait_recv()
        value = t_got[c, 0]
        for i in range(1, n_head):
            value = value + t_got[c, i]
        a = 1.0 / jnp.sqrt(value[:CHUNK] / width_all + EPSILON)
        scale_a[c, 0:CHUNK] = a
        scale_b[c, 0:CHUNK] = a * a * (a * value[CHUNK:] / width_all)

    for c in range(n_chunks - 1, 0, -1):
        gather_part(c)

        @pl.loop(0, CHUNK // pair)
        def _(i):
            top = c * CHUNK + CHUNK - 1 - i * pair
            back_states([top - u for u in range(pair)], both_heads)

    gather_part(0)
    for h in both_heads:

        @pl.loop(0, CHUNK // pair)
        def _(i):
            top = CHUNK - 1 - i * pair
            back_states([top - u for u in range(pair)], [h])

        scatter(h, r_run, r_got, r_send, r_recv)

    def inner_back(g):
        before = before_gate(g)
        for h in both_heads:
            dp_t[h] = (dot(v_n[h, g], dob_t[h, g]) * mask_ref[g]).astype(BF16)
        for h in both_heads:
            dv_t[h, g] = dot(dob_t[h, g], p_t[h, g], 1, 1)
        out_v[g] = join(0, [o_t[h, g] * wide(scale_a, g) for h in both_heads])
        more = [dot(s_bf[h, g], dob_t[h, g] * before, 0, 0) for h in both_heads]
        dq_v[g] = join(1, [dot(k_t[h, g], dp_t[h]) + more[h] for h in both_heads])
        for h in both_heads:
            dk_t[h, g] = dot(q_t[h, g], dp_t[h], 1, 1)

    cut1, cut2 = (2 * n_groups) // 3, (5 * n_groups) // 6

    @pl.loop(0, cut1)
    def _(g):
        inner_back(g)

    combine(0, r_run, r_got, r_pre, r_in, r_send, r_recv, True)
    give(0, r_pre, r_in, u_send, u_recv)

    @pl.loop(cut1, cut2)
    def _(g):
        inner_back(g)

    for h in range(1, n_heads):
        combine(h, r_run, r_got, r_pre, r_in, r_send, r_recv, True)
        give(h, r_pre, r_in, u_send, u_recv)

    @pl.loop(cut2, n_groups)
    def _(g):
        inner_back(g)

    for h in both_heads:
        sends_done(h, s_run, s_got, s_send, s_recv, s_pre, s_in, t_send, t_recv)
    for c in range(n_chunks):
        for d in head_order:
            part_copy(c, d, False).wait_send()
    for h in both_heads:
        give_done(h, r_in, u_send, u_recv)
        sends_done(h, r_run, r_got, r_send, r_recv, r_pre, r_in, u_send, u_recv)


def last_kernel(
    sizes,
    doc_ref,
    out_v,
    dq_v,
    dk_t,
    dv_t,
    k_t,
    v_t,
    r_loc,
    r_in,
    out_hbm,
    dq_hbm,
    dk_hbm,
    dv_hbm,
    stage,
    done,
    sem,
    whole,
):
    n_seq, n_x, n_y, n_groups, n_heads = sizes
    tokens = n_groups * GROUP
    shard_first = lax.axis_index("seq") * tokens
    copies = [
        pltpu.make_async_copy(out_v, out_hbm, whole.at[0]),
        pltpu.make_async_copy(dq_v, dq_hbm, whole.at[1]),
    ]
    for c in copies:
        c.start()
    ends = doc_ends(doc_ref)
    after_s = seg_of(ends, shard_first + tokens)
    targets = (dk_hbm, dv_hbm)
    pair = 2

    def store(i, g):
        return pltpu.make_async_copy(done.at[i, g], targets[i].at[g], sem.at[i, g])

    @pl.loop(0, n_groups // pair)
    def _(step):
        todo = []
        for u in range(pair):
            g = step * pair + u
            first = shard_first + g * GROUP
            w = flag(seg_of(ends, first + GROUP) == after_s)
            after = lane_gate(True, last_end(ends, first + GROUP) - first)
            for h in range(n_heads):
                state = (r_loc[h, g + 1] + w * r_in[h]).astype(BF16)
                todo.append((0, u, g, h, dk_t, dot(state, v_t[h, g] * after)))
                todo.append((1, u, g, h, dv_t, dot(state, k_t[h, g] * after, 0, 0)))
        for i, u, g, h, base, x in todo:
            block = (base[h, g] + x).astype(BF16).T.astype(F32)
            stage[2 * u + i, pl.ds(h, GROUP, stride=n_heads), :] = block
        for u in range(pair):
            for i in range(2):
                g = step * pair + u
                done[i, g] = stage[2 * u + i].astype(BF16)
                store(i, g).start()

    @pl.loop(0, n_groups)
    def _(g):
        for i in range(2):
            store(i, g).wait()

    for c in copies:
        c.wait()


def per_device(sizes, queries, keys, values, cotangent, doc_lengths):
    tokens_here, n_heads, width = queries.shape
    n_seq, n_x, n_y = sizes
    n_groups = tokens_here // GROUP
    n_chunks = n_groups // CHUNK
    rows2 = GROUP * n_heads
    slab = width // n_seq
    sizes = (n_seq, n_x, n_y, n_groups, n_heads)
    view = lambda x: x.reshape(n_groups, rows2, width)
    dma = pltpu.SemaphoreType.DMA
    vm = pltpu.VMEM
    anywhere = pl.BlockSpec(memory_space=pl.ANY)
    on_chip = pl.BlockSpec(memory_space=pltpu.VMEM)
    scalars = pl.BlockSpec(memory_space=pltpu.SMEM)
    per_head = (n_heads, n_groups, GROUP, width)
    turned = (n_heads, n_groups, width, GROUP)
    states = (n_heads, n_groups + 1, width, width)
    one_state = (n_heads, width, width)
    slices = (n_heads, n_seq, slab, width)
    sums = (n_chunks, 2 * CHUNK, GROUP)
    packed = (n_groups, rows2, width)
    mids = pl.pallas_call(
        functools.partial(main_kernel, sizes),
        out_shape=(
            vm(packed, BF16),
            vm(packed, BF16),
            vm(turned, F32),
            vm(turned, F32),
            vm(turned, BF16),
            vm(turned, BF16),
            vm(states, F32),
            vm(one_state, F32),
        ),
        in_specs=[scalars] + [anywhere] * 4,
        out_specs=(on_chip,) * 8,
        scratch_shapes=[
            vm((4,) + packed, BF16),
            vm((4, rows2, width), F32),
            vm(per_head, BF16),
            vm(per_head, BF16),
            vm(turned, BF16),
            vm(turned, BF16),
            vm((n_groups, GROUP, GROUP), F32),
            vm((n_heads, n_groups, GROUP, GROUP), BF16),
            vm((n_heads, GROUP, GROUP), BF16),
            vm(turned, F32),
            vm(turned, BF16),
            vm((2, rows2, width), F32),
            vm(states, F32),
            vm((n_heads, n_groups, width, width), BF16),
            pltpu.SMEM((2, n_seq), F32),
            vm(slices, F32),
            vm(slices, F32),
            vm(one_state, F32),
            vm(slices, F32),
            vm(slices, F32),
            vm(sums, F32),
            vm((n_chunks, n_x * n_y, 2 * CHUNK, GROUP), F32),
            vm(sums, F32),
            vm(sums, F32),
            dma((4, n_groups)),
        ]
        + [dma((n_heads, n_seq))] * 8
        + [dma((n_chunks, n_x * n_y))] * 2,
        compiler_params=pltpu.CompilerParams(
            collective_id=0, has_side_effects=True, vmem_limit_bytes=44 << 20
        ),
        name="exchange_and_attend",
    )(doc_lengths, view(queries), view(keys), view(values), view(cotangent))
    mids = [pltpu.with_memory_space_constraint(m, pltpu.VMEM) for m in mids]
    results = pl.pallas_call(
        functools.partial(last_kernel, sizes),
        out_shape=(jax.ShapeDtypeStruct(packed, BF16),) * 4,
        in_specs=[scalars] + [on_chip] * 8,
        out_specs=(anywhere,) * 4,
        scratch_shapes=[
            vm((4, rows2, width), F32),
            vm((2,) + packed, BF16),
            dma((2, n_groups)),
            dma((2,)),
        ],
        compiler_params=pltpu.CompilerParams(vmem_limit_bytes=16 << 20),
        name="finish",
    )(doc_lengths, *mids)
    return tuple(r.reshape(tokens_here, n_heads, width) for r in results)


def solution(mesh):
    n_x = 4
    spec = P("seq", "head", None)
    return jax.shard_map(
        functools.partial(per_device, (mesh.shape["seq"], n_x, mesh.shape["head"] // n_x)),
        mesh=mesh,
        in_specs=(spec,) * 4 + (P(),),
        out_specs=(spec,) * 4,
        check_vma=False,
    )
```

time: 65.3 us -> 50.2 us (0.77)
  Pallas kernels: 64.5 us -> 49.5 us
    pallas_call x1, Pallas kernels: 59.9 us -> 45.5 us  [per_device(): pl.pallas_call(functools.partial(main_kernel, sizes), out_shape=(vm(packe...]
where the time goes in v3:
time: 50.2 us; the launch traced here: 50.1 us
  Pallas kernels  49.5 us (99%)
  between operations  0.66 us (1%)
    pallas_call x1, Pallas kernels, per_device(): pl.pallas_call(functools.partial(main_kernel, sizes), out_shape=(vm(packe...  45.5 us
    pallas_call x1, Pallas kernels, per_device(): pl.pallas_call(functools.partial(last_kernel, sizes), out_shape=(jax.Shap...  4.01 us

profile of v3, /device:TPU:1, one launch (start us, length us, event | category | flops | bytes accessed | tf_op | source)
XLA Modules:
  0.0 50.1 jit_solution(13047448061684341888)
XLA Ops:
  0.6 0.0 copy-start
  0.6 45.5 %exchange_and_attend.1 = (bf16[12,512,128]{2,1,0:T(8,128)(2,1)S(1)}, bf16[12,512,128]{2,1,0:T(8,128)(2,1)S(1)}, f32[2,12,128,256]{3,2,1,0:T(8,128)S(1)}, f32[2,1...) custom-call(s32[6]{0:T(128)} %doc_ref.3, ...), custom_call_target="tpu_custom_call" | custom-call | tf_op jit(solution)/shard_map/exchange_and_attend/pallas_call | solution.py:588
  46.1 0.0 copy-done
  46.1 4.0 %finish.1 = (bf16[12,512,128]{2,1,0:T(8,128)(2,1)}, bf16[12,512,128]{2,1,0:T(8,128)(2,1)}, bf16[12,512,128]{2,1,0:T(8,128)(2,1)}, bf16[12,512,128]{2,1,0:T(8,128)(2,1)}) custom-call(s32[6]{0:T(128)S(1)} %copy-done, bf16[12,512,128]{2,1,0:T(8,128)(2,1)S(1)} %get-tuple-element.16.out_v, bf16[12,512,128]{2,1,0:T(8,128)(2,1)S(1)} %get-tuple-element.17.dq_v, ...), custom_call_target="tpu_custom_call" | custom-call | tf_op jit(solution)/shard_map/finish/pallas_call | solution.py:637
Async XLA Ops:
  0.6 45.5 %copy-start = (s32[6]{0:T(128)S(1)}, s32[6]{0:T(128)}, u32[]{:S(2)}) copy-start(s32[6]{0:T(128)} %doc_ref.3) | copy-start | bytes 76

commit v4 on v3

--- a/solution.py
+++ b/solution.py
@@ -72,23 +72,26 @@
 
 def main_kernel(
     sizes,
-    doc_ref,
+    doc_hbm,
     q_hbm,
     k_hbm,
     v_hbm,
     g_hbm,
     out_v,
     dq_v,
-    dk_t,
-    dv_t,
-    k_t,
-    v_t,
+    dk_part,
+    dv_part,
+    k_after,
+    v_after,
+    weight,
     r_loc,
     r_in,
     raw,
     tmp,
     k_n,
     v_n,
+    k_t,
+    v_t,
     q_t,
     g_t,
     mask_ref,
@@ -100,6 +103,7 @@
     s_loc,
     s_bf,
     keep_ref,
+    doc_ref,
     s_got,
     s_pre,
     s_in,
@@ -120,6 +124,7 @@
     u_recv,
     a_send,
     a_recv,
+    doc_sem,
 ):
     n_seq, n_x, n_y, n_groups, n_heads = sizes
     tokens = n_groups * GROUP
@@ -145,6 +150,8 @@
         y = lax.rem(my + n_y + sign * (d // n_x), n_y)
         return y * n_x + x
 
+    doc_copy = pltpu.make_async_copy(doc_hbm, doc_ref, doc_sem)
+    doc_copy.start()
     sources = (k_hbm, v_hbm, q_hbm, g_hbm)
 
     def load(a, g):
@@ -166,8 +173,10 @@
     for d in head_order:
         pl.semaphore_signal(barrier, inc=1, device_id={"head": head_peer(d, 1)}, device_id_type=MESH)
 
+    doc_copy.wait()
     ends = doc_ends(doc_ref)
     shard_first = me * tokens
+    after_s = seg_of(ends, shard_first + tokens)
     bs = seg_of(ends, shard_first - 1)
 
     def edges(g):
@@ -202,6 +211,10 @@
             stage[slot, pl.ds(h, GROUP, stride=n_heads), :] = parts[h].astype(BF16).T.astype(F32)
         return stage[slot].astype(BF16)
 
+    def put(ref, g, parts):
+        for h in both_heads:
+            ref[g, pl.ds(h, GROUP, stride=n_heads), :] = parts[h].astype(F32).T
+
     def key_states(groups, h):
         added = [dot(v_t[h, g] * tail_gate(g), k_n[h, g]) for g in groups]
         for g, new in zip(groups, added):
@@ -212,21 +225,14 @@
         return pltpu.make_async_remote_copy(
             src_ref=src,
             dst_ref=dst,
-            send_sem=send.at[d],
-            recv_sem=recv.at[me],
+            send_sem=send,
+            recv_sem=recv,
             device_id={"seq": seq_peer(d)},
             device_id_type=MESH,
         )
 
-    def taken(dst, send, recv, d):
-        return pltpu.make_async_remote_copy(
-            src_ref=dst,
-            dst_ref=dst,
-            send_sem=send.at[d],
-            recv_sem=recv.at[seq_peer(d)],
-            device_id={"seq": seq_peer(d)},
-            device_id_type=MESH,
-        )
+    def everything(got, h, send, recv):
+        return hand(got.at[h, pl.ds(0, n_seq - 1)], got.at[h, pl.ds(0, n_seq - 1)], send, recv, 1)
 
     def rows(ref, h, i):
         return ref.at[h, pl.ds(pl.multiple_of(i * slab, slab), slab)]
@@ -252,8 +258,7 @@
     def combine(h, run, got, pre, into, send, recv, backward):
         mine = pl.ds(pl.multiple_of(me * slab, slab), slab)
         got[h, me] = run.ref[h, run.slot, mine, :]
-        for d in reversed(seq_order):
-            taken(got.at[h, seq_peer(d)], send.at[h], recv.at[h], d).wait_recv()
+        everything(got, h, send.at[h], recv.at[h]).wait_recv()
         carry = jnp.zeros((slab, 128), F32)
         for i in range(n_seq - 1, -1, -1) if backward else range(n_seq):
             pre[h, i] = carry
@@ -264,14 +269,12 @@
         for d in seq_order:
             hand(pre.at[h, seq_peer(d)], rows(into, h, me), send.at[h], recv.at[h], d).start()
 
-    def give_done(h, into, send, recv):
-        for d in reversed(seq_order):
-            taken(rows(into, h, seq_peer(d)), send.at[h], recv.at[h], d).wait_recv()
-
-    def sends_done(h, run, got, send, recv, pre, into, send2, recv2):
-        for d in seq_order:
-            hand(rows(run, h, seq_peer(d)), got.at[h, me], send.at[h], recv.at[h], d).wait_send()
-            hand(pre.at[h, seq_peer(d)], rows(into, h, me), send2.at[h], recv2.at[h], d).wait_send()
+    def give_done(h, got, send, recv):
+        everything(got, h, send.at[h], recv.at[h]).wait_recv()
+
+    def sends_done(h, got, *pairs):
+        for send, recv in pairs:
+            everything(got, h, send.at[h], recv.at[h]).wait_send()
 
     pair = 2
     for h in both_heads:
@@ -380,25 +383,34 @@
                 part[c, two, :] += inner
 
     for h in range(n_heads - 1):
-        give_done(h, s_in, t_send, t_recv)
+        give_done(h, s_pre, t_send, t_recv)
 
         @pl.loop(0, n_pairs)
         def _(i):
             outer([i * pair + u for u in range(pair)], h)
 
-    give_done(n_heads - 1, s_in, t_send, t_recv)
-
-    def part_copy(c, d, wait):
-        slot = head_peer(d, 1) if wait else head
+    give_done(n_heads - 1, s_pre, t_send, t_recv)
+
+    def part_copy(c, d):
         return pltpu.make_async_remote_copy(
             src_ref=part.at[c],
-            dst_ref=t_got.at[c, slot],
-            send_sem=a_send.at[c, d],
-            recv_sem=a_recv.at[c, slot],
+            dst_ref=t_got.at[c, head],
+            send_sem=a_send.at[c],
+            recv_sem=a_recv.at[c],
             device_id={"head": head_peer(d, 1)},
             device_id_type=MESH,
         )
 
+    def all_parts(c):
+        return pltpu.make_async_remote_copy(
+            src_ref=t_got.at[c, pl.ds(0, n_head - 1)],
+            dst_ref=t_got.at[c, pl.ds(0, n_head - 1)],
+            send_sem=a_send.at[c],
+            recv_sem=a_recv.at[c],
+            device_id={"head": head_peer(1, 1)},
+            device_id_type=MESH,
+        )
+
     for c in range(n_chunks - 1, -1, -1):
 
         @pl.loop(0, CHUNK // pair)
@@ -406,7 +418,7 @@
             outer([c * CHUNK + i * pair + u for u in range(pair)], n_heads - 1)
 
         for d in head_order:
-            part_copy(c, d, False).start()
+            part_copy(c, d).start()
         t_got[c, head] = part[c]
 
     for h in both_heads:
@@ -427,8 +439,7 @@
                 r_loc[h, g] = flag(c0 == ac) * r_loc[h, g + 1] + new
 
     def gather_part(c):
-        for d in reversed(head_order):
-            part_copy(c, d, True).wait_recv()
+        all_parts(c).wait_recv()
         value = t_got[c, 0]
         for i in range(1, n_head):
             value = value + t_got[c, i]
@@ -456,15 +467,21 @@
 
     def inner_back(g):
         before = before_gate(g)
+        bc, c0, c1, ac = edges(g)
+        weight[g] = jnp.broadcast_to(flag(ac == after_s), (8, 128))
+        first = shard_first + g * GROUP
+        row = lax.broadcasted_iota(jnp.int32, (GROUP, 128), 0)
+        after = jnp.where(row >= last_end(ends, first + GROUP) - first, 1.0, 0.0).astype(BF16)
         for h in both_heads:
             dp_t[h] = (dot(v_n[h, g], dob_t[h, g]) * mask_ref[g]).astype(BF16)
-        for h in both_heads:
-            dv_t[h, g] = dot(dob_t[h, g], p_t[h, g], 1, 1)
+        put(dv_part, g, [dot(dob_t[h, g], p_t[h, g], 1, 1) for h in both_heads])
         out_v[g] = join(0, [o_t[h, g] * wide(scale_a, g) for h in both_heads])
         more = [dot(s_bf[h, g], dob_t[h, g] * before, 0, 0) for h in both_heads]
         dq_v[g] = join(1, [dot(k_t[h, g], dp_t[h]) + more[h] for h in both_heads])
+        put(dk_part, g, [dot(q_t[h, g], dp_t[h], 1, 1) for h in both_heads])
         for h in both_heads:
-            dk_t[h, g] = dot(q_t[h, g], dp_t[h], 1, 1)
+            k_after[h, g] = k_n[h, g] * after
+            v_after[h, g] = v_n[h, g] * after
 
     cut1, cut2 = (2 * n_groups) // 3, (5 * n_groups) // 6
 
@@ -488,24 +505,23 @@
         inner_back(g)
 
     for h in both_heads:
-        sends_done(h, s_run, s_got, s_send, s_recv, s_pre, s_in, t_send, t_recv)
+        sends_done(h, s_pre, (s_send, s_recv), (t_send, t_recv), (r_send, r_recv))
     for c in range(n_chunks):
-        for d in head_order:
-            part_copy(c, d, False).wait_send()
+        all_parts(c).wait_send()
     for h in both_heads:
-        give_done(h, r_in, u_send, u_recv)
-        sends_done(h, r_run, r_got, r_send, r_recv, r_pre, r_in, u_send, u_recv)
+        give_done(h, r_pre, u_send, u_recv)
+        sends_done(h, r_pre, (u_send, u_recv))
 
 
 def last_kernel(
     sizes,
-    doc_ref,
     out_v,
     dq_v,
-    dk_t,
-    dv_t,
-    k_t,
-    v_t,
+    dk_part,
+    dv_part,
+    k_after,
+    v_after,
+    weight,
     r_loc,
     r_in,
     out_hbm,
@@ -518,41 +534,31 @@
     whole,
 ):
     n_seq, n_x, n_y, n_groups, n_heads = sizes
-    tokens = n_groups * GROUP
-    shard_first = lax.axis_index("seq") * tokens
     copies = [
         pltpu.make_async_copy(out_v, out_hbm, whole.at[0]),
         pltpu.make_async_copy(dq_v, dq_hbm, whole.at[1]),
     ]
     for c in copies:
         c.start()
-    ends = doc_ends(doc_ref)
-    after_s = seg_of(ends, shard_first + tokens)
     targets = (dk_hbm, dv_hbm)
-    pair = 2
+    parts = (dk_part, dv_part)
+    batch = 4
 
     def store(i, g):
         return pltpu.make_async_copy(done.at[i, g], targets[i].at[g], sem.at[i, g])
 
-    @pl.loop(0, n_groups // pair)
+    @pl.loop(0, n_groups // batch)
     def _(step):
-        todo = []
-        for u in range(pair):
-            g = step * pair + u
-            first = shard_first + g * GROUP
-            w = flag(seg_of(ends, first + GROUP) == after_s)
-            after = lane_gate(True, last_end(ends, first + GROUP) - first)
+        for u in range(batch):
+            g = step * batch + u
+            w = jnp.broadcast_to(weight[g, 0:1, :], (128, 128))
             for h in range(n_heads):
                 state = (r_loc[h, g + 1] + w * r_in[h]).astype(BF16)
-                todo.append((0, u, g, h, dk_t, dot(state, v_t[h, g] * after)))
-                todo.append((1, u, g, h, dv_t, dot(state, k_t[h, g] * after, 0, 0)))
-        for i, u, g, h, base, x in todo:
-            block = (base[h, g] + x).astype(BF16).T.astype(F32)
-            stage[2 * u + i, pl.ds(h, GROUP, stride=n_heads), :] = block
-        for u in range(pair):
+                even = pl.ds(h, GROUP, stride=n_heads)
+                stage[2 * u, even, :] = dot(v_after[h, g], state, 1, 1)
+                stage[2 * u + 1, even, :] = dot(k_after[h, g], state)
             for i in range(2):
-                g = step * pair + u
-                done[i, g] = stage[2 * u + i].astype(BF16)
+                done[i, g] = (stage[2 * u + i] + parts[i][g]).astype(BF16)
                 store(i, g).start()
 
     @pl.loop(0, n_groups)
@@ -577,7 +583,6 @@
     vm = pltpu.VMEM
     anywhere = pl.BlockSpec(memory_space=pl.ANY)
     on_chip = pl.BlockSpec(memory_space=pltpu.VMEM)
-    scalars = pl.BlockSpec(memory_space=pltpu.SMEM)
     per_head = (n_heads, n_groups, GROUP, width)
     turned = (n_heads, n_groups, width, GROUP)
     states = (n_heads, n_groups + 1, width, width)
@@ -590,20 +595,23 @@
         out_shape=(
             vm(packed, BF16),
             vm(packed, BF16),
-            vm(turned, F32),
-            vm(turned, F32),
-            vm(turned, BF16),
-            vm(turned, BF16),
+            vm(packed, F32),
+            vm(packed, F32),
+            vm(per_head, BF16),
+            vm(per_head, BF16),
+            vm((n_groups, 8, 128), F32),
             vm(states, F32),
             vm(one_state, F32),
         ),
-        in_specs=[scalars] + [anywhere] * 4,
-        out_specs=(on_chip,) * 8,
+        in_specs=[anywhere] * 5,
+        out_specs=(on_chip,) * 9,
         scratch_shapes=[
             vm((4,) + packed, BF16),
             vm((4, rows2, width), F32),
             vm(per_head, BF16),
             vm(per_head, BF16),
+            vm(turned, BF16),
+            vm(turned, BF16),
             vm(turned, BF16),
             vm(turned, BF16),
             vm((n_groups, GROUP, GROUP), F32),
@@ -615,6 +623,7 @@
             vm(states, F32),
             vm((n_heads, n_groups, width, width), BF16),
             pltpu.SMEM((2, n_seq), F32),
+            pltpu.SMEM(doc_lengths.shape, jnp.int32),
             vm(slices, F32),
             vm(slices, F32),
             vm(one_state, F32),
@@ -626,8 +635,9 @@
             vm(sums, F32),
             dma((4, n_groups)),
         ]
-        + [dma((n_heads, n_seq))] * 8
-        + [dma((n_chunks, n_x * n_y))] * 2,
+        + [dma((n_heads,))] * 8
+        + [dma((n_chunks,))] * 2
+        + [dma],
         compiler_params=pltpu.CompilerParams(
             collective_id=0, has_side_effects=True, vmem_limit_bytes=44 << 20
         ),
@@ -637,17 +647,17 @@
     results = pl.pallas_call(
         functools.partial(last_kernel, sizes),
         out_shape=(jax.ShapeDtypeStruct(packed, BF16),) * 4,
-        in_specs=[scalars] + [on_chip] * 8,
+        in_specs=[on_chip] * 9,
         out_specs=(anywhere,) * 4,
         scratch_shapes=[
-            vm((4, rows2, width), F32),
+            vm((8, rows2, width), F32),
             vm((2,) + packed, BF16),
             dma((2, n_groups)),
             dma((2,)),
         ],
         compiler_params=pltpu.CompilerParams(vmem_limit_bytes=16 << 20),
         name="finish",
-    )(doc_lengths, *mids)
+    )(*mids)
     return tuple(r.reshape(tokens_here, n_heads, width) for r in results)
 
 

time: 50.2 us -> 46.2 us (0.920)
  Pallas kernels: 49.5 us -> 45.4 us
    pallas_call x1, Pallas kernels: 45.5 us -> 42.6 us  [per_device(): pl.pallas_call(functools.partial(main_kernel, sizes), out_shape=(vm(packe...]
    pallas_call x1, Pallas kernels: 4.01 us -> 2.86 us  [per_device(): pl.pallas_call(functools.partial(last_kernel, sizes), out_shape=(jax.Shap...]
where the time goes in v4:
time: 46.2 us; the launch traced here: 46.1 us
  Pallas kernels  45.4 us (98%)
  between operations  0.64 us (1%)
    pallas_call x1, Pallas kernels, per_device(): pl.pallas_call(functools.partial(main_kernel, sizes), out_shape=(vm(packe...  42.6 us
    pallas_call x1, Pallas kernels, per_device(): pl.pallas_call(functools.partial(last_kernel, sizes), out_shape=(jax.Shap...  2.86 us

profile of v4, /device:TPU:1, one launch (start us, length us, event | category | flops | bytes accessed | tf_op | source)
XLA Modules:
  0.0 46.1 jit_solution(17268331314725274584)
XLA Ops:
  0.6 42.6 %exchange_and_attend.1 = (bf16[12,512,128]{2,1,0:T(8,128)(2,1)S(1)}, bf16[12,512,128]{2,1,0:T(8,128)(2,1)S(1)}, f32[12,512,128]{2,1,0:T(8,128)S(1)}, f32[12,512,...) custom-call(s32[6]{0:T(128)} %doc_hbm.1, ...), custom_call_target="tpu_custom_call" | custom-call | tf_op jit(solution)/shard_map/exchange_and_attend/pallas_call | solution.py:593
  43.2 2.9 %finish.1 = (bf16[12,512,128]{2,1,0:T(8,128)(2,1)}, bf16[12,512,128]{2,1,0:T(8,128)(2,1)}, bf16[12,512,128]{2,1,0:T(8,128)(2,1)}, bf16[12,512,128]{2,1,0:T(8,128)(2,1)}) custom-call(bf16[12,512,128]{2,1,0:T(8,128)(2,1)S(1)} %get-tuple-element.17.out_v, bf16[12,512,128]{2,1,0:T(8,128)(2,1)S(1)} %get-tuple-element.18.dq_v, ...), custom_call_target="tpu_custom_call" | custom-call | tf_op jit(solution)/shard_map/finish/pallas_call | solution.py:647

commit v5 on v4

--- a/solution.py
+++ b/solution.py
@@ -154,18 +154,21 @@
     doc_copy.start()
     sources = (k_hbm, v_hbm, q_hbm, g_hbm)
 
+    pair = 2
+
     def load(a, g):
-        return pltpu.make_async_copy(sources[a].at[g], raw.at[a, g], in_sem.at[a, g])
-
-    @pl.loop(0, n_groups)
-    def _(g):
-        load(0, g).start()
-        load(1, g).start()
-
-    @pl.loop(0, n_groups)
-    def _(g):
-        load(2, g).start()
-        load(3, g).start()
+        two = pl.ds(g, pair)
+        return pltpu.make_async_copy(sources[a].at[two], raw.at[a, two], in_sem.at[a, g // pair])
+
+    @pl.loop(0, n_groups // pair)
+    def _(i):
+        load(0, i * pair).start()
+        load(1, i * pair).start()
+
+    @pl.loop(0, n_groups // pair)
+    def _(i):
+        load(2, i * pair).start()
+        load(3, i * pair).start()
 
     barrier = pltpu.get_barrier_semaphore()
     for d in seq_order:
@@ -276,23 +279,27 @@
         for send, recv in pairs:
             everything(got, h, send.at[h], recv.at[h]).wait_send()
 
-    pair = 2
     for h in both_heads:
         s_loc[h, 0] = jnp.zeros((128, 128), F32)
 
-    @pl.loop(0, n_groups // pair)
-    def _(i):
-        groups = [i * pair + u for u in range(pair)]
-        for g in groups:
-            load(0, g).wait()
-            load(1, g).wait()
+    def batch(i):
+        return [i * CHUNK + u for u in range(CHUNK)]
+
+    def take_keys_values(groups):
+        for half in range(CHUNK // pair):
+            load(0, groups[half * pair]).wait()
+            load(1, groups[half * pair]).wait()
         for u, g in enumerate(groups):
-            for h, x in enumerate(spread(0, g, 2 * u)):
-                k_n[h, g] = x
             for h, x in enumerate(spread(1, g, 2 * u + 1)):
                 v_n[h, g] = x
                 v_t[h, g] = x.T
-        key_states(groups, 0)
+            for h, x in enumerate(spread(0, g, 2 * u)):
+                k_n[h, g] = x
+
+    @pl.loop(0, n_groups // CHUNK)
+    def _(i):
+        take_keys_values(batch(i))
+        key_states(batch(i), 0)
 
     pl.semaphore_wait(barrier, n_seq - 1 + n_head - 1)
     scatter(0, s_run, s_got, s_send, s_recv)
@@ -301,7 +308,7 @@
 
         @pl.loop(0, n_groups // CHUNK)
         def _(i):
-            key_states([i * CHUNK + u for u in range(CHUNK)], h)
+            key_states(batch(i), h)
 
         scatter(h, s_run, s_got, s_send, s_recv)
 
@@ -320,8 +327,8 @@
 
     def intra(i):
         groups = [i * pair + u for u in range(pair)]
+        load(2, groups[0]).wait()
         for u, g in enumerate(groups):
-            load(2, g).wait()
             build_mask(g)
             for h, x in enumerate(spread(2, g, u)):
                 q_t[h, g] = x.T
@@ -334,34 +341,29 @@
                 o_t[h, g] = dot(v_t[h, g], p_t[h, g])
 
     n_pairs = n_groups // pair
-    cut1, cut2 = (2 * n_pairs) // 3, (5 * n_pairs) // 6
-
-    @pl.loop(0, cut1)
+
+    def take_cotangent(groups):
+        for half in range(CHUNK // pair):
+            load(3, groups[half * pair]).wait()
+        for u, g in enumerate(groups):
+            for h, x in enumerate(spread(3, g, u)):
+                g_t[h, g] = x.T
+
+    @pl.loop(0, n_pairs - 1)
     def _(i):
         intra(i)
 
-    combine(0, s_run, s_got, s_pre, s_in, s_send, s_recv, False)
-    give(0, s_pre, s_in, t_send, t_recv)
-
-    @pl.loop(cut1, cut2)
-    def _(i):
-        intra(i)
-
-    for h in range(1, n_heads):
+    for h in both_heads:
         combine(h, s_run, s_got, s_pre, s_in, s_send, s_recv, False)
         give(h, s_pre, s_in, t_send, t_recv)
-
-    @pl.loop(cut2, n_pairs)
+        if h == 0:
+            take_cotangent(batch(0))
+
+    intra(n_pairs - 1)
+
+    @pl.loop(1, n_groups // CHUNK)
     def _(i):
-        intra(i)
-
-    @pl.loop(0, n_pairs)
-    def _(i):
-        groups = [i * pair + u for u in range(pair)]
-        for u, g in enumerate(groups):
-            load(3, g).wait()
-            for h, x in enumerate(spread(3, g, u)):
-                g_t[h, g] = x.T
+        take_cotangent(batch(i))
 
     def outer(groups, h):
         for g in groups:
@@ -385,9 +387,9 @@
     for h in range(n_heads - 1):
         give_done(h, s_pre, t_send, t_recv)
 
-        @pl.loop(0, n_pairs)
+        @pl.loop(0, n_groups // CHUNK)
         def _(i):
-            outer([i * pair + u for u in range(pair)], h)
+            outer([i * CHUNK + u for u in range(CHUNK)], h)
 
     give_done(n_heads - 1, s_pre, t_send, t_recv)
 
@@ -413,9 +415,7 @@
 
     for c in range(n_chunks - 1, -1, -1):
 
-        @pl.loop(0, CHUNK // pair)
-        def _(i):
-            outer([c * CHUNK + i * pair + u for u in range(pair)], n_heads - 1)
+        outer([c * CHUNK + u for u in range(CHUNK)], n_heads - 1)
 
         for d in head_order:
             part_copy(c, d).start()
@@ -450,18 +450,12 @@
     for c in range(n_chunks - 1, 0, -1):
         gather_part(c)
 
-        @pl.loop(0, CHUNK // pair)
-        def _(i):
-            top = c * CHUNK + CHUNK - 1 - i * pair
-            back_states([top - u for u in range(pair)], both_heads)
+        back_states([c * CHUNK + CHUNK - 1 - u for u in range(CHUNK)], both_heads)
 
     gather_part(0)
     for h in both_heads:
 
-        @pl.loop(0, CHUNK // pair)
-        def _(i):
-            top = CHUNK - 1 - i * pair
-            back_states([top - u for u in range(pair)], [h])
+        back_states([CHUNK - 1 - u for u in range(CHUNK)], [h])
 
         scatter(h, r_run, r_got, r_send, r_recv)
 
@@ -483,7 +477,7 @@
             k_after[h, g] = k_n[h, g] * after
             v_after[h, g] = v_n[h, g] * after
 
-    cut1, cut2 = (2 * n_groups) // 3, (5 * n_groups) // 6
+    cut1, cut2 = n_groups // 2, n_groups // 2 + 1
 
     @pl.loop(0, cut1)
     def _(g):
@@ -607,7 +601,7 @@
         out_specs=(on_chip,) * 9,
         scratch_shapes=[
             vm((4,) + packed, BF16),
-            vm((4, rows2, width), F32),
+            vm((8, rows2, width), F32),
             vm(per_head, BF16),
             vm(per_head, BF16),
             vm(turned, BF16),
@@ -633,7 +627,7 @@
             vm((n_chunks, n_x * n_y, 2 * CHUNK, GROUP), F32),
             vm(sums, F32),
             vm(sums, F32),
-            dma((4, n_groups)),
+            dma((4, n_groups // 2)),
         ]
         + [dma((n_heads,))] * 8
         + [dma((n_chunks,))] * 2

time: 46.2 us -> 44.5 us (0.963)
  Pallas kernels: 45.4 us -> 43.7 us
    pallas_call x1, Pallas kernels: 42.6 us -> 40.9 us  [per_device(): pl.pallas_call(functools.partial(main_kernel, sizes), out_shape=(vm(packe...]
where the time goes in v5:
time: 44.5 us; the launch traced here: 44.4 us
  Pallas kernels  43.7 us (98%)
  between operations  0.64 us (1%)
    pallas_call x1, Pallas kernels, per_device(): pl.pallas_call(functools.partial(main_kernel, sizes), out_shape=(vm(packe...  40.9 us
    pallas_call x1, Pallas kernels, per_device(): pl.pallas_call(functools.partial(last_kernel, sizes), out_shape=(jax.Shap...  2.86 us

profile of v5, /device:TPU:1, one launch (start us, length us, event | category | flops | bytes accessed | tf_op | source)
XLA Modules:
  0.0 44.4 jit_solution(2354082319100502566)
XLA Ops:
  0.6 40.9 %exchange_and_attend.1 = (bf16[12,512,128]{2,1,0:T(8,128)(2,1)S(1)}, bf16[12,512,128]{2,1,0:T(8,128)(2,1)S(1)}, f32[12,512,128]{2,1,0:T(8,128)S(1)}, f32[12,512,...) custom-call(s32[6]{0:T(128)} %doc_hbm.1, ...), custom_call_target="tpu_custom_call" | custom-call | tf_op jit(solution)/shard_map/exchange_and_attend/pallas_call | solution.py:587
  41.5 2.9 %finish.1 = (bf16[12,512,128]{2,1,0:T(8,128)(2,1)}, bf16[12,512,128]{2,1,0:T(8,128)(2,1)}, bf16[12,512,128]{2,1,0:T(8,128)(2,1)}, bf16[12,512,128]{2,1,0:T(8,128)(2,1)}) custom-call(bf16[12,512,128]{2,1,0:T(8,128)(2,1)S(1)} %get-tuple-element.17.out_v, bf16[12,512,128]{2,1,0:T(8,128)(2,1)S(1)} %get-tuple-element.18.dq_v, ...), custom_call_target="tpu_custom_call" | custom-call | tf_op jit(solution)/shard_map/finish/pallas_call | solution.py:641

commit v6 on v5

--- a/solution.py
+++ b/solution.py
@@ -102,6 +102,9 @@
     stage,
     s_loc,
     s_bf,
+    q_before,
+    q_lead,
+    table,
     keep_ref,
     doc_ref,
     s_got,
@@ -349,27 +352,39 @@
             for h, x in enumerate(spread(3, g, u)):
                 g_t[h, g] = x.T
 
-    @pl.loop(0, n_pairs - 1)
+    early = (2 * n_pairs) // 3
+
+    @pl.loop(0, early)
     def _(i):
         intra(i)
 
-    for h in both_heads:
+    combine(0, s_run, s_got, s_pre, s_in, s_send, s_recv, False)
+    give(0, s_pre, s_in, t_send, t_recv)
+    intra(early)
+    for h in range(1, n_heads):
         combine(h, s_run, s_got, s_pre, s_in, s_send, s_recv, False)
         give(h, s_pre, s_in, t_send, t_recv)
-        if h == 0:
-            take_cotangent(batch(0))
-
-    intra(n_pairs - 1)
-
-    @pl.loop(1, n_groups // CHUNK)
+    for i in range(early + 1, n_pairs):
+        intra(i)
+
+    @pl.loop(0, n_groups // CHUNK)
     def _(i):
         take_cotangent(batch(i))
 
+    @pl.loop(0, n_groups)
+    def _(g):
+        bc, c0, c1, ac = edges(g)
+        table[0, g] = flag(bc == bs)
+        table[1, g] = flag(c0 == ac)
+        before, lead = before_gate(g), lead_gate(g)
+        for h in both_heads:
+            q_before[h, g] = q_t[h, g] * before
+            q_lead[h, g] = q_t[h, g] * lead
+
     def outer(groups, h):
         for g in groups:
-            bc, c0, c1, ac = edges(g)
-            s_bf[h, g] = (s_loc[h, g] + flag(bc == bs) * s_in[h]).astype(BF16)
-        more = [dot(s_bf[h, g], q_t[h, g] * before_gate(g)) for g in groups]
+            s_bf[h, g] = (s_loc[h, g] + table[0, g] * s_in[h]).astype(BF16)
+        more = [dot(s_bf[h, g], q_before[h, g]) for g in groups]
         for g, x in zip(groups, more):
             o = o_t[h, g] + x
             o_t[h, g] = o
@@ -432,11 +447,10 @@
         for g in groups:
             for h in heads:
                 dob_t[h, g] = (g_t[h, g].astype(F32) * wide(scale_a, g) - o_t[h, g] * wide(scale_b, g)).astype(BF16)
-        added = [[dot(q_t[h, g] * lead_gate(g), dob_t[h, g], 1, 1) for h in heads] for g in groups]
+        added = [[dot(q_lead[h, g], dob_t[h, g], 1, 1) for h in heads] for g in groups]
         for g, row in zip(groups, added):
-            bc, c0, c1, ac = edges(g)
             for h, new in zip(heads, row):
-                r_loc[h, g] = flag(c0 == ac) * r_loc[h, g + 1] + new
+                r_loc[h, g] = table[1, g] * r_loc[h, g + 1] + new
 
     def gather_part(c):
         all_parts(c).wait_recv()
@@ -477,7 +491,7 @@
             k_after[h, g] = k_n[h, g] * after
             v_after[h, g] = v_n[h, g] * after
 
-    cut1, cut2 = n_groups // 2, n_groups // 2 + 1
+    cut1 = n_groups // 2
 
     @pl.loop(0, cut1)
     def _(g):
@@ -486,15 +500,11 @@
     combine(0, r_run, r_got, r_pre, r_in, r_send, r_recv, True)
     give(0, r_pre, r_in, u_send, u_recv)
 
-    @pl.loop(cut1, cut2)
-    def _(g):
-        inner_back(g)
-
     for h in range(1, n_heads):
         combine(h, r_run, r_got, r_pre, r_in, r_send, r_recv, True)
         give(h, r_pre, r_in, u_send, u_recv)
 
-    @pl.loop(cut2, n_groups)
+    @pl.loop(cut1, n_groups)
     def _(g):
         inner_back(g)
 
@@ -536,13 +546,12 @@
         c.start()
     targets = (dk_hbm, dv_hbm)
     parts = (dk_part, dv_part)
-    batch = 4
+    batch = 12
 
     def store(i, g):
         return pltpu.make_async_copy(done.at[i, g], targets[i].at[g], sem.at[i, g])
 
-    @pl.loop(0, n_groups // batch)
-    def _(step):
+    for step in range(n_groups // batch):
         for u in range(batch):
             g = step * batch + u
             w = jnp.broadcast_to(weight[g, 0:1, :], (128, 128))
@@ -616,6 +625,9 @@
             vm((2, rows2, width), F32),
             vm(states, F32),
             vm((n_heads, n_groups, width, width), BF16),
+            vm(turned, BF16),
+            vm(turned, BF16),
+            pltpu.SMEM((2, n_groups), F32),
             pltpu.SMEM((2, n_seq), F32),
             pltpu.SMEM(doc_lengths.shape, jnp.int32),
             vm(slices, F32),
@@ -644,7 +656,7 @@
         in_specs=[on_chip] * 9,
         out_specs=(anywhere,) * 4,
         scratch_shapes=[
-            vm((8, rows2, width), F32),
+            vm((24, rows2, width), F32),
             vm((2,) + packed, BF16),
             dma((2, n_groups)),
             dma((2,)),

time: 44.5 us -> 44.7 us (level)
  no operation moved by 1% of the time
where the time goes in v6:
time: 44.7 us
  Pallas kernels  44 us (98%)
  between operations  0.64 us (1%)
    pallas_call x1, Pallas kernels, per_device(): pl.pallas_call(functools.partial(main_kernel, sizes), out_shape=(vm(packe...  40.8 us
    pallas_call x1, Pallas kernels, per_device(): pl.pallas_call(functools.partial(last_kernel, sizes), out_shape=(jax.Shap...  3.2 us

profile of v6, /device:TPU:1, one launch (start us, length us, event | category | flops | bytes accessed | tf_op | source)
XLA Modules:
  0.0 44.7 jit_solution(1508939193303029133)
XLA Ops:
  0.6 40.8 %exchange_and_attend.1 = (bf16[12,512,128]{2,1,0:T(8,128)(2,1)S(1)}, bf16[12,512,128]{2,1,0:T(8,128)(2,1)S(1)}, f32[12,512,128]{2,1,0:T(8,128)S(1)}, f32[12,512,...) custom-call(s32[6]{0:T(128)} %doc_hbm.1, ...), custom_call_target="tpu_custom_call" | custom-call | tf_op jit(solution)/shard_map/exchange_and_attend/pallas_call | solution.py:596
  41.4 3.2 %finish.1 = (bf16[12,512,128]{2,1,0:T(8,128)(2,1)}, bf16[12,512,128]{2,1,0:T(8,128)(2,1)}, bf16[12,512,128]{2,1,0:T(8,128)(2,1)}, bf16[12,512,128]{2,1,0:T(8,128)(2,1)}) custom-call(bf16[12,512,128]{2,1,0:T(8,128)(2,1)S(1)} %get-tuple-element.17.out_v, bf16[12,512,128]{2,1,0:T(8,128)(2,1)S(1)} %get-tuple-element.18.dq_v, ...), custom_call_target="tpu_custom_call" | custom-call | tf_op jit(solution)/shard_map/finish/pallas_call | solution.py:653

commit v7 on v6

--- a/solution.py
+++ b/solution.py
@@ -302,17 +302,11 @@
     @pl.loop(0, n_groups // CHUNK)
     def _(i):
         take_keys_values(batch(i))
-        key_states(batch(i), 0)
+        for h in both_heads:
+            key_states(batch(i), h)
 
     pl.semaphore_wait(barrier, n_seq - 1 + n_head - 1)
-    scatter(0, s_run, s_got, s_send, s_recv)
-
-    for h in range(1, n_heads):
-
-        @pl.loop(0, n_groups // CHUNK)
-        def _(i):
-            key_states(batch(i), h)
-
+    for h in both_heads:
         scatter(h, s_run, s_got, s_send, s_recv)
 
     for i in range(n_seq):
@@ -354,18 +348,15 @@
 
     early = (2 * n_pairs) // 3
 
-    @pl.loop(0, early)
+    @pl.loop(0, n_pairs)
     def _(i):
         intra(i)
 
-    combine(0, s_run, s_got, s_pre, s_in, s_send, s_recv, False)
-    give(0, s_pre, s_in, t_send, t_recv)
-    intra(early)
-    for h in range(1, n_heads):
-        combine(h, s_run, s_got, s_pre, s_in, s_send, s_recv, False)
-        give(h, s_pre, s_in, t_send, t_recv)
-    for i in range(early + 1, n_pairs):
-        intra(i)
+        @pl.when(i == early - 1)
+        def _():
+            for h in both_heads:
+                combine(h, s_run, s_got, s_pre, s_in, s_send, s_recv, False)
+                give(h, s_pre, s_in, t_send, t_recv)
 
     @pl.loop(0, n_groups // CHUNK)
     def _(i):
@@ -428,10 +419,10 @@
             device_id_type=MESH,
         )
 
-    for c in range(n_chunks - 1, -1, -1):
-
-        outer([c * CHUNK + u for u in range(CHUNK)], n_heads - 1)
-
+    @pl.loop(0, n_chunks)
+    def _(i):
+        c = n_chunks - 1 - i
+        outer(batch(c), n_heads - 1)
         for d in head_order:
             part_copy(c, d).start()
         t_got[c, head] = part[c]
@@ -461,16 +452,13 @@
         scale_a[c, 0:CHUNK] = a
         scale_b[c, 0:CHUNK] = a * a * (a * value[CHUNK:] / width_all)
 
-    for c in range(n_chunks - 1, 0, -1):
+    @pl.loop(0, n_chunks)
+    def _(i):
+        c = n_chunks - 1 - i
         gather_part(c)
-
-        back_states([c * CHUNK + CHUNK - 1 - u for u in range(CHUNK)], both_heads)
-
-    gather_part(0)
+        back_states(batch(c)[::-1], both_heads)
+
     for h in both_heads:
-
-        back_states([CHUNK - 1 - u for u in range(CHUNK)], [h])
-
         scatter(h, r_run, r_got, r_send, r_recv)
 
     def inner_back(g):
@@ -491,22 +479,15 @@
             k_after[h, g] = k_n[h, g] * after
             v_after[h, g] = v_n[h, g] * after
 
-    cut1 = n_groups // 2
-
-    @pl.loop(0, cut1)
+    @pl.loop(0, n_groups)
     def _(g):
         inner_back(g)
 
-    combine(0, r_run, r_got, r_pre, r_in, r_send, r_recv, True)
-    give(0, r_pre, r_in, u_send, u_recv)
-
-    for h in range(1, n_heads):
-        combine(h, r_run, r_got, r_pre, r_in, r_send, r_recv, True)
-        give(h, r_pre, r_in, u_send, u_recv)
-
-    @pl.loop(cut1, n_groups)
-    def _(g):
-        inner_back(g)
+        @pl.when(g == n_groups // 2 - 1)
+        def _():
+            for h in both_heads:
+                combine(h, r_run, r_got, r_pre, r_in, r_send, r_recv, True)
+                give(h, r_pre, r_in, u_send, u_recv)
 
     for h in both_heads:
         sends_done(h, s_pre, (s_send, s_recv), (t_send, t_recv), (r_send, r_recv))
@@ -546,12 +527,13 @@
         c.start()
     targets = (dk_hbm, dv_hbm)
     parts = (dk_part, dv_part)
-    batch = 12
+    batch = 4
 
     def store(i, g):
         return pltpu.make_async_copy(done.at[i, g], targets[i].at[g], sem.at[i, g])
 
-    for step in range(n_groups // batch):
+    @pl.loop(0, n_groups // batch)
+    def _(step):
         for u in range(batch):
             g = step * batch + u
             w = jnp.broadcast_to(weight[g, 0:1, :], (128, 128))
@@ -656,7 +638,7 @@
         in_specs=[on_chip] * 9,
         out_specs=(anywhere,) * 4,
         scratch_shapes=[
-            vm((24, rows2, width), F32),
+            vm((8, rows2, width), F32),
             vm((2,) + packed, BF16),
             dma((2, n_groups)),
             dma((2,)),

time: 44.7 us -> 45.1 us (level)
    pallas_call x1, Pallas kernels: 40.8 us -> 41.5 us  [per_device(): pl.pallas_call(functools.partial(main_kernel, sizes), out_shape=(vm(packe...]
where the time goes in v7:
time: 45.1 us; the launch traced here: 45 us
  Pallas kernels  44.4 us (98%)
  between operations  0.64 us (1%)
    pallas_call x1, Pallas kernels, per_device(): pl.pallas_call(functools.partial(main_kernel, sizes), out_shape=(vm(packe...  41.5 us
    pallas_call x1, Pallas kernels, per_device(): pl.pallas_call(functools.partial(last_kernel, sizes), out_shape=(jax.Shap...  2.86 us

profile of v7, /device:TPU:1, one launch (start us, length us, event | category | flops | bytes accessed | tf_op | source)
XLA Modules:
  0.0 45.0 jit_solution(14672493045778807552)
XLA Ops:
  0.6 41.5 %exchange_and_attend.1 = (bf16[12,512,128]{2,1,0:T(8,128)(2,1)S(1)}, bf16[12,512,128]{2,1,0:T(8,128)(2,1)S(1)}, f32[12,512,128]{2,1,0:T(8,128)S(1)}, f32[12,512,...) custom-call(s32[6]{0:T(128)} %doc_hbm.1, ...), custom_call_target="tpu_custom_call" | custom-call | tf_op jit(solution)/shard_map/exchange_and_attend/pallas_call | solution.py:578
  42.1 2.9 %finish.1 = (bf16[12,512,128]{2,1,0:T(8,128)(2,1)}, bf16[12,512,128]{2,1,0:T(8,128)(2,1)}, bf16[12,512,128]{2,1,0:T(8,128)(2,1)}, bf16[12,512,128]{2,1,0:T(8,128)(2,1)}) custom-call(bf16[12,512,128]{2,1,0:T(8,128)(2,1)S(1)} %get-tuple-element.17.out_v, bf16[12,512,128]{2,1,0:T(8,128)(2,1)S(1)} %get-tuple-element.18.dq_v, ...), custom_call_target="tpu_custom_call" | custom-call | tf_op jit(solution)/shard_map/finish/pallas_call | solution.py:635
